TPU v7x, 256 devices: a whole 4x4x8 slice. The times are simulated.
256 devices in a mesh: grp: 8 (over x, core), tile: 32 (over z, y).
Axes of the slice: x: 4, y: 4, z: 8, core: 2. Of those that a mesh axis runs over, the one named last changes fastest.
Arguments:
- tx_fields: bfloat16 [64, 32768], P(None, 'tile'), may hold values from -6 to 6
- rx_fields: bfloat16 [128, 32768], P(None, 'tile'), may hold values from -6 to 6
- layer_of_cell: int32 [32768], P('tile'), may hold values from 0 to 31
- layer_cond: float32 [32], replicated, may hold values from 0.05 to 5
- tx_of_row: int32 [2816], replicated, may hold values from 0 to 63
- rx_of_row: int32 [2816], replicated, may hold values from 0 to 127
- damping: float32 [2816], replicated, may hold values from 0.5 to 5
- panel_order: int32 [2816], replicated, may hold values from 0 to 2815, each once
Outputs:
- trailing: float32 [2816, 2816], P('grp', 'tile')
- factor: float32 [2816, 1024], P('grp')
Inputs may be any that keep to these rules, and one draw needn't show every extreme that they name: `panel_order`: each data row appears exactly once; panel k is entries k * 512 to (k + 1) * 512 - 1.
All inputs are finite; a program needn't handle non-finite values.
Results may differ from a plain program's by a relative error of at most 0.0014.
Values may be sent and summed in bfloat16 or wider, within the bound.
A program may use at most 64 MiB of HBM per device.

v0:
```python
import jax
import jax.numpy as jnp
from jax import lax
from jax.sharding import PartitionSpec as P

PANEL = 512
NPAN = 2


highest = lax.Precision.HIGHEST


def from_root(value, axis, source):
    kept = jnp.where(lax.axis_index(axis) == source, value, 0).astype(value.dtype)
    return lax.psum(kept, axis)


def shards(
    tx_fields, rx_fields, layer_of_cell, layer_cond, tx_of_row, rx_of_row, damping, panel_order
):
    grp_count = lax.axis_size("grp")
    tile_count = lax.axis_size("tile")
    tile_cells = tx_fields.shape[1]
    total_rows = tx_of_row.shape[0]
    group_rows = total_rows // grp_count
    tile_cols = total_rows // tile_count
    group_start = lax.axis_index("grp") * group_rows
    tile_start = lax.axis_index("tile") * tile_cols
    levels = jnp.arange(layer_cond.shape[0], dtype=jnp.int32)
    layer_hot = (levels[:, None] == layer_of_cell[None, :]).astype(jnp.float32)
    cell_cond = jnp.dot(layer_cond[None, :], layer_hot, precision=highest)[0]
    contract = (((1,), (1,)), ((), ()))
    product = (
        jnp.take(
            tx_fields, lax.dynamic_slice_in_dim(tx_of_row, group_start, group_rows), axis=0
        ).astype(jnp.float32)
        * jnp.take(
            rx_fields, lax.dynamic_slice_in_dim(rx_of_row, group_start, group_rows), axis=0
        ).astype(jnp.float32)
        * cell_cond[None, :]
    )
    sens_own = product.astype(jnp.bfloat16)
    block_cols = lax.psum_scatter(
        lax.dot_general(
            lax.all_gather(sens_own, "grp", axis=0, tiled=True),
            sens_own,
            contract,
            preferred_element_type=jnp.float32,
        ),
        "tile",
        scatter_dimension=0,
        tiled=True,
    )
    cell_total = tile_cells * tile_count
    row_ids = group_start + jnp.arange(group_rows, dtype=jnp.int32)
    col_ids = tile_start + jnp.arange(tile_cols, dtype=jnp.int32)
    on_diagonal = row_ids[:, None] == col_ids[None, :]
    damp_rows = lax.dynamic_slice_in_dim(damping, group_start, group_rows)
    trailing = block_cols.T / cell_total + jnp.where(on_diagonal, damp_rows[:, None], 0.0)
    factor_parts = []
    for turn_index in range(NPAN):
        chosen = panel_order[turn_index * PANEL : (turn_index + 1) * PANEL]
        col_pick = (col_ids[:, None] == chosen[None, :]).astype(jnp.float32)
        row_pick = (chosen[:, None] == row_ids[None, :]).astype(jnp.float32)
        columns = lax.psum(jnp.dot(trailing, col_pick, precision=highest), "tile")
        diag_block = lax.psum(jnp.dot(row_pick, columns, precision=highest), "grp")
        block_factor = jnp.linalg.cholesky(diag_block)
        panel_factor = lax.linalg.triangular_solve(
            block_factor, columns, left_side=False, lower=True, transpose_a=True
        )
        owner_index = lax.axis_index("tile") * tile_cols // group_rows
        owned_rows = lax.dynamic_slice_in_dim(
            panel_factor, tile_start - owner_index * group_rows, tile_cols, 0
        )
        column_factor = from_root(owned_rows, "grp", owner_index)
        trailing = trailing - jnp.dot(panel_factor, column_factor.T, precision=highest)
        factor_parts.append(panel_factor)
    return (trailing, jnp.concatenate(factor_parts, axis=1))


def solution(mesh):
    placed = (P(None, "tile"), P(None, "tile"), P("tile"), P(), P(), P(), P(), P())
    return jax.shard_map(
        shards,
        mesh=mesh,
        in_specs=placed,
        out_specs=(P("grp", "tile"), P("grp", None)),
        check_vma=False,
    )
```

profile of v0, /device:TPU:16, one launch (start us, length us, event | category | flops | bytes accessed | tf_op | source)
XLA Modules:
  0.0 1140.8 jit_solution(2589747190513932107)
XLA Ops:
  15.5 44.1 %all-gather.2.cloned.1.call-done = bf16[2816,1024]{1,0:T(8,128)(2,1)} async-done(((bf16[352,1024]{1,0:T(8,128)(2,1)}), bf16[2816,1024]{1,0:T(8,128)(2,1)}) %all-gather.2.cloned.1.call-update) | async-done | bytes 5767184 | tf_op jit(solution)/shard_map/all_gather | solution.py:45
  69.2 211.2 %reduce-scatter.4.cloned.1.call-done = f32[88,352]{1,0:T(8,128)} async-done(((f32[2816,352]{1,0:T(8,128)}), f32[88,352]{1,0:T(8,128)}) %reduce-scatter.4.cloned.1.call-update) | async-done | bytes 123920
  282.8 149.2 %all-reduce.9.cloned.1.call-done = f32[352,512]{1,0:T(8,128)} async-done(((f32[352,512]{1,0:T(8,128)}), f32[352,512]{1,0:T(8,128)}) %all-reduce.9.cloned.1.call-update) | async-done | bytes 720912 | tf_op jit(solution)/shard_map/psum | solution.py:65
  435.7 65.7 %all-reduce.11.cloned.1.call-done = f32[512,512]{0,1:T(8,128)} async-done(((f32[512,512]{0,1:T(8,128)}), f32[512,512]{0,1:T(8,128)}) %all-reduce.11.cloned.1.call-update) | async-done | bytes 1048592 | tf_op jit(solution)/shard_map/psum | solution.py:66
  503.3 11.7 %cholesky.286 = f32[128,128]{1,0:T(8,128)S(1)} custom-call(f32[128,128]{1,0:T(8,128)S(1)} %cholesky.426), custom_call_target="Cholesky" | custom-call | tf_op jit(solution)/shard_map/jit(cholesky)/cholesky | solution.py:67
  515.2 9.8 custom-call.27
  525.7 11.7 %cholesky.305 = f32[128,128]{1,0:T(8,128)S(1)} custom-call(f32[128,128]{1,0:T(8,128)S(1)} %cholesky.430), custom_call_target="Cholesky" | custom-call | tf_op jit(solution)/shard_map/jit(cholesky)/cholesky | solution.py:67
  538.7 10.0 custom-call.28
  549.4 11.7 %cholesky.326 = f32[128,128]{1,0:T(8,128)S(1)} custom-call(f32[128,128]{1,0:T(8,128)S(1)} %cholesky.435), custom_call_target="Cholesky" | custom-call | tf_op jit(solution)/shard_map/jit(cholesky)/cholesky | solution.py:67
  561.8 9.8 custom-call.29
  572.2 11.7 %cholesky.343 = f32[128,128]{1,0:T(8,128)S(1)} custom-call(f32[128,128]{1,0:T(8,128)S(1)} %convolution_subtract_fusion.13), custom_call_target="Cholesky" | custom-call | tf_op jit(solution)/shard_map/jit(cholesky)/cholesky | solution.py:67
  595.7 39.3 %custom-call.30 = f32[4,128,128]{1,2,0:T(8,128)S(1)} custom-call(f32[4,128,128]{2,1,0:T(8,128)S(1)} %get-tuple-element.18), custom_call_target="InvertDiagBlocksLowerTriangular" | custom-call | tf_op jit(solution)/shard_map/triangular_solve/custom-call.3 | solution.py:68
  638.5 64.7 %all-reduce.13.cloned.1.call-done = f32[88,512]{1,0:T(8,128)} async-done(((f32[88,512]{1,0:T(8,128)}), f32[88,512]{1,0:T(8,128)}) %all-reduce.13.cloned.1.call-update) | async-done | bytes 180240 | tf_op jit(solution)/shard_map/psum | solution.py:15
  706.4 148.0 %all-reduce.15.cloned.1.call-done = f32[352,512]{1,0:T(8,128)} async-done(((f32[352,512]{1,0:T(8,128)}), f32[352,512]{1,0:T(8,128)}) %all-reduce.15.cloned.1.call-update) | async-done | bytes 720912 | tf_op jit(solution)/shard_map/psum | solution.py:65
  858.0 65.8 %all-reduce.17.cloned.1.call-done = f32[512,512]{0,1:T(8,128)} async-done(((f32[512,512]{0,1:T(8,128)}), f32[512,512]{0,1:T(8,128)}) %all-reduce.17.cloned.1.call-update) | async-done | bytes 1048592 | tf_op jit(solution)/shard_map/psum | solution.py:66
  926.7 11.7 %cholesky.358 = f32[128,128]{1,0:T(8,128)S(1)} custom-call(f32[128,128]{1,0:T(8,128)S(1)} %cholesky.439), custom_call_target="Cholesky" | custom-call | tf_op jit(solution)/shard_map/jit(cholesky)/cholesky | solution.py:67
  938.6 9.8 custom-call.31
  950.9 11.7 %cholesky.377 = f32[128,128]{1,0:T(8,128)S(1)} custom-call(f32[128,128]{1,0:T(8,128)S(1)} %cholesky.443), custom_call_target="Cholesky" | custom-call | tf_op jit(solution)/shard_map/jit(cholesky)/cholesky | solution.py:67
  964.0 9.9 custom-call.32
  975.5 11.7 %cholesky.398 = f32[128,128]{1,0:T(8,128)S(1)} custom-call(f32[128,128]{1,0:T(8,128)S(1)} %cholesky.448), custom_call_target="Cholesky" | custom-call | tf_op jit(solution)/shard_map/jit(cholesky)/cholesky | solution.py:67
  987.9 9.8 custom-call.33
  999.2 11.7 %cholesky.415 = f32[128,128]{1,0:T(8,128)S(1)} custom-call(f32[128,128]{1,0:T(8,128)S(1)} %convolution_subtract_fusion.12), custom_call_target="Cholesky" | custom-call | tf_op jit(solution)/shard_map/jit(cholesky)/cholesky | solution.py:67
  1023.0 39.3 %custom-call.34 = f32[4,128,128]{1,2,0:T(8,128)S(1)} custom-call(f32[4,128,128]{2,1,0:T(8,128)S(1)} %get-tuple-element.19), custom_call_target="InvertDiagBlocksLowerTriangular" | custom-call | tf_op jit(solution)/shard_map/triangular_solve/custom-call.3 | solution.py:68
  1067.9 63.6 %all-reduce.19.cloned.1.call-done = f32[88,512]{1,0:T(8,128)} async-done(((f32[88,512]{1,0:T(8,128)}), f32[88,512]{1,0:T(8,128)}) %all-reduce.19.cloned.1.call-update) | async-done | bytes 180240 | tf_op jit(solution)/shard_map/psum | solution.py:15
  (157 shorter events, 93.5 us)
Async XLA Ops:
  7.2 4.7 copy-start
  7.2 52.4 %all-gather.2.cloned.1.call-start = ((), (), s32[]{:S(2)}) async-start(), calls=%async_computation.1 | async-start | bytes 6488064 | tf_op jit(solution)/shard_map/all_gather | solution.py:45
  11.8 2.1 copy-start.14
  11.8 2.1 copy-start.15
  15.4 264.9 %reduce-scatter.4.cloned.1.call-start = ((), (), s32[]{:S(2)}) async-start(), calls=%async_computation.8 | async-start | bytes 4460544
  67.6 364.3 %all-reduce.9.cloned.1.call-start = ((), (), s32[]{:S(2)}) async-start(), calls=%async_computation.2 | async-start | bytes 1441792 | tf_op jit(solution)/shard_map/psum | solution.py:65
  282.7 218.7 %all-reduce.11.cloned.1.call-start = ((), (), s32[]{:S(2)}) async-start(), calls=%async_computation.3 | async-start | bytes 2097152 | tf_op jit(solution)/shard_map/psum | solution.py:66
  435.2 268.1 %all-reduce.13.cloned.1.call-start = ((), (), s32[]{:S(2)}) async-start(), calls=%async_computation.4 | async-start | bytes 360448 | tf_op jit(solution)/shard_map/psum | solution.py:15
  501.4 1.7 copy-start.1
  587.3 47.8 %copy-start.3 = (f32[352,512]{1,0:T(8,128)S(1)}, f32[352,512]{1,0:T(8,128)}, u32[]{:S(2)}) copy-start(f32[352,512]{1,0:T(8,128)} %all-reduce.9.cloned.1.call-done) | copy-start | bytes 2162692
  636.7 66.5 %copy-start.5 = (f32[352,128]{1,0:T(8,128)}, f32[352,128]{1,0:T(8,128)S(1)}, u32[]{:S(2)}) copy-start(f32[352,128]{1,0:T(8,128)S(1)} %fusion.67) | copy-start | bytes 540676
  637.4 65.9 %copy-start.11 = (f32[88,352]{1,0:T(8,128)S(1)}, f32[88,352]{1,0:T(8,128)}, u32[]{:S(2)}) copy-start(f32[88,352]{1,0:T(8,128)} %reduce-scatter.4.cloned.1.call-done) | copy-start | bytes 371716
  637.7 67.2 %copy-start.8 = (f32[352,128]{1,0:T(8,128)}, f32[352,128]{1,0:T(8,128)S(1)}, u32[]{:S(2)}) copy-start(f32[352,128]{1,0:T(8,128)S(1)} %fusion.66) | copy-start | bytes 540676
  638.5 215.9 %all-reduce.15.cloned.1.call-start = ((), (), s32[]{:S(2)}) async-start(), calls=%async_computation.5 | async-start | bytes 1441792 | tf_op jit(solution)/shard_map/psum | solution.py:65
  704.9 152.7 %copy-start.12 = (f32[352,88]{0,1:T(8,128)}, f32[352,88]{0,1:T(8,128)S(1)}, u32[]{:S(2)}) copy-start(f32[352,88]{0,1:T(8,128)S(1)} %convolution_subtract_fusion.9) | copy-start | bytes 371716
  706.3 217.5 %all-reduce.17.cloned.1.call-start = ((), (), s32[]{:S(2)}) async-start(), calls=%async_computation.6 | async-start | bytes 2097152 | tf_op jit(solution)/shard_map/psum | solution.py:66
  857.6 273.8 %all-reduce.19.cloned.1.call-start = ((), (), s32[]{:S(2)}) async-start(), calls=%async_computation.7 | async-start | bytes 360448 | tf_op jit(solution)/shard_map/psum | solution.py:15
  923.8 1.7 copy-start.2
  925.7 1.0 copy-start.7
  1014.1 48.2 %copy-start.4 = (f32[352,512]{1,0:T(8,128)S(1)}, f32[352,512]{1,0:T(8,128)}, u32[]{:S(2)}) copy-start(f32[352,512]{1,0:T(8,128)} %all-reduce.15.cloned.1.call-done) | copy-start | bytes 2162692
  1062.3 1.7 copy-start.10
  1064.6 2.0 copy-start.6
  1064.7 2.0 copy-start.9
  1066.7 64.8 %copy-start.13 = (f32[352,88]{0,1:T(8,128)S(1)}, f32[352,88]{0,1:T(8,128)}, u32[]{:S(2)}) copy-start(f32[352,88]{0,1:T(8,128)} %copy-done.12) | copy-start | bytes 371716
Sparse Core Ops, SparseCore 0:
  15.6 43.9 all-gather.1
  67.7 212.5 reduce-scatter.3
  284.4 147.5 all-reduce.8
  435.3 66.0 all-reduce.10
  638.6 64.6 all-reduce.12
  707.1 147.2 all-reduce.14
  857.7 66.0 all-reduce.16
  1066.8 64.6 all-reduce.18
where the time goes:
time: 1150 us; the launch traced here: 1140 us
  waiting for transfers between devices  812 us (71%)
  other arithmetic  243 us (21%)
  matrix products  35.7 us (3%)
  local copies, waits for them, and re-layouts  28.4 us (2%)
  between operations  20.2 us (2%)
    psum x2, waiting for transfers between devices, shards(): columns = lax.psum(jnp.dot(trailing, col_pick, precision=highest), 'tile')  297 us
    unnamed x9, waiting for transfers between devices  211 us
    another operation x30, other arithmetic, shards(): block_factor = jnp.linalg.cholesky(diag_block)  158 us
    psum x2, waiting for transfers between devices, shards(): diag_block = lax.psum(jnp.dot(row_pick, columns, precision=highest), 'grp')  131 us
    psum x2, waiting for transfers between devices, from_root(): return lax.psum(kept, axis)  128 us
    another operation x7, other arithmetic, shards(): lax.linalg.triangular_solve(block_factor, columns, left_side=False, lower...  79.4 us
    all_gather x1, waiting for transfers between devices, shards(): lax.all_gather(sens_own, 'grp', axis=0, tiled=True)  44.1 us
  transfers between devices with their start and end apart: 8, of which 8 were waited for; matrix products, arithmetic and copies ran while one was open for 0% of the time, Pallas kernels for 0%

commit v1 on v0

v1 whole, which is shorter than its diff:
```python
import functools

import jax
import jax.numpy as jnp
from jax import lax
from jax.experimental import pallas as pl
from jax.experimental.pallas import tpu as pltpu
from jax.sharding import PartitionSpec as P

F32 = jnp.float32
BF16 = jnp.bfloat16
MESH = pl.DeviceIdType.MESH
VMEM = pltpu.VMEM
DMA = pltpu.SemaphoreType.DMA

M = 2816
NCELLS = 32768
PICKED = 1024
NX, NY, NZ, NCORE = 4, 4, 8, 2
NG = NX * NCORE
NT = NY * NZ
ROWS = M // NG
COLS = M // NT
PG = PICKED // NG
PT = PICKED // NT
CELLS = NCELLS // NT
RIGHT = 512
LEFT = COLS + PT
B = 128


def dot(a, b, ca, cb):
    return lax.dot_general(a, b, (((ca,), (cb,)), ((), ())), preferred_element_type=F32)


def split(x):
    hi = x.astype(BF16)
    return hi, (x - hi.astype(F32)).astype(BF16)


def places():
    g = lax.axis_index("grp")
    t = lax.axis_index("tile")
    return g // NCORE, g % NCORE, t // NY, t % NY


def at_z(z, y):
    return {"tile": lax.rem(z + NZ, NZ) * NY + y}


def greet(peers):
    barrier = pltpu.get_barrier_semaphore()
    for peer in peers:
        pl.semaphore_signal(barrier, inc=1, device_id=peer, device_id_type=MESH)
    pl.semaphore_wait(barrier, len(peers))


def sends(src, dst, send, recv, peer):
    return pltpu.make_async_remote_copy(
        src_ref=src, dst_ref=dst, send_sem=send, recv_sem=recv, device_id=peer, device_id_type=MESH
    )


def owner_of(z, i):
    hops = (i + 1) // 2
    return lax.rem(z + NZ + jnp.where(i % 2 == 1, -hops, hops), NZ)


def gram_kernel(
    fields_ref, cond_ref, tx_hot_ref, rx_hot_ref, out_ref, held, conds, sens,
    ring_send, ring_recv, cond_send, cond_recv, pair_send, pair_recv, local,
):
    x, c, z, y = places()
    up, down, pair = at_z(z + 1, y), at_z(z + NZ - 1, y), {"grp": x * NCORE + 1 - c}
    greet((up, down, pair))

    def ring(i, peer, first):
        o = z if first else owner_of(z, i - 2)
        half = fields_ref.at[c] if first else held.at[o, c]
        line = cond_ref if first else conds.at[o]
        return (
            sends(half, held.at[o, c], ring_send.at[i], ring_recv.at[i], peer),
            sends(line, conds.at[o], cond_send.at[i], cond_recv.at[i], peer),
        )

    def to_pair(i):
        o = owner_of(z, i)
        return sends(held.at[o, c], held.at[o, c], pair_send.at[i], pair_recv.at[i], pair)

    def start(copies):
        for copy in copies:
            copy.start()

    start(ring(1, up, True))
    start(ring(2, down, True))
    mine = pltpu.make_async_copy(fields_ref, held.at[z], local.at[0])
    mine_line = pltpu.make_async_copy(cond_ref, conds.at[z], local.at[1])
    mine.start()
    mine_line.start()
    out_ref[...] = jnp.zeros_like(out_ref)
    mine.wait()
    mine_line.wait()

    def arrive(i, peer, onward):
        for copy in ring(i, peer, False):
            copy.wait_recv()
        to_pair(i).start()
        if onward is not None:
            start(ring(i + 2, onward, False))

    def body(i, carry):
        @pl.when((i % 2 == 1) & (i < 6))
        def _():
            for copy in ring(i + 2, up, False):
                copy.wait_recv()
            to_pair(i + 2).start()

        @pl.when((i % 2 == 1) & (i < 4))
        def _():
            start(ring(i + 4, up, False))

        @pl.when((i % 2 == 0) & (i < 6))
        def _():
            for copy in ring(i + 2, down, False):
                copy.wait_recv()
            to_pair(i + 2).start()

        @pl.when((i % 2 == 0) & (i < 4))
        def _():
            start(ring(i + 4, down, False))

        @pl.when(i >= 1)
        def _():
            to_pair(i).wait_recv()

        o = owner_of(z, i)
        width = 256

        def chunk(j, carry):
            at = pl.ds(pl.multiple_of(j * width, width), width)
            txs = held[o, 0, 0:64, at]
            rxs = jnp.concatenate([held[o, 0, 64:96, at], held[o, 1, :, at]], axis=0)
            part = dot(tx_hot_ref[...], txs, 1, 0) * dot(rx_hot_ref[...], rxs, 1, 0)
            sens[:, at] = (part * conds[o, :, at]).astype(BF16)
            return carry

        lax.fori_loop(0, CELLS // width, chunk, 0)
        out_ref[...] += dot(sens[RIGHT:, :], sens[0:RIGHT, :], 1, 1)
        return carry

    for copy in ring(1, up, True):
        copy.wait_recv()
    to_pair(1).start()
    start(ring(3, up, False))
    lax.fori_loop(0, NZ, body, 0)

    for i in range(1, NZ):
        for copy in ring(i, up if i % 2 == 1 else down, i < 3):
            copy.wait_send()
        to_pair(i).wait_send()


def gram_sums(fields, cond, tx_hot, rx_hot):
    vmem = pl.BlockSpec(memory_space=VMEM)
    return pl.pallas_call(
        gram_kernel,
        out_shape=jax.ShapeDtypeStruct((NY * LEFT, RIGHT), F32),
        in_specs=[vmem] * 4,
        out_specs=vmem,
        scratch_shapes=[
            VMEM((NZ, NCORE, 96, CELLS), BF16),
            VMEM((NZ, 1, CELLS), F32),
            VMEM((RIGHT + NY * LEFT, CELLS), BF16),
        ]
        + [DMA((NZ,))] * 6
        + [DMA((2,))],
        compiler_params=pltpu.CompilerParams(
            collective_id=0, has_side_effects=True, vmem_limit_bytes=40 << 20
        ),
        name="gram_sums",
    )(fields, cond, tx_hot, rx_hot)


def spread_kernel(
    part_ref, damp_ref, own_ref, rows_ref, diag_ref, cross_ref, got, own,
    sum_send, sum_recv, y_send, y_recv, ring_send, ring_recv,
    x_send, x_recv, pair_send, pair_recv, ex_send, ex_recv, ep_send, ep_recv, local,
):
    x, c, z, y = places()
    g = x * NCORE + c
    up, down, pair = at_z(z + 1, y), at_z(z + NZ - 1, y), {"grp": x * NCORE + 1 - c}
    at_y = [None] + [{"tile": z * NY + lax.rem(y + d, NY)} for d in range(1, NY)]
    at_x = [None] + [{"grp": lax.rem(x + d, NX) * NCORE + c} for d in range(1, NX)]
    greet(at_y[1:] + at_x[1:] + [up, down, pair])

    sums = [
        sends(part_ref.at[lax.rem(y + d, NY)], got.at[d], sum_send.at[d], sum_recv.at[d], at_y[d])
        for d in range(1, NY)
    ]
    for copy in sums:
        copy.start()
    total = part_ref[y]
    for d, copy in enumerate(sums, 1):
        copy.wait_recv()
        total += got[d]
    own[...] = total * (1.0 / NCELLS) + damp_ref[...]

    picked = own.at[COLS:LEFT, :]
    crossed = own.at[0:COLS, 0:PG]
    ys = [sends(picked, rows_ref.at[z, y], y_send.at[d], y_recv.at[d], at_y[d]) for d in range(1, NY)]
    for copy in ys:
        copy.start()
    mine = [
        pltpu.make_async_copy(picked, rows_ref.at[z, y], local.at[0]),
        pltpu.make_async_copy(crossed, cross_ref.at[g], local.at[1]),
        pltpu.make_async_copy(own, own_ref, local.at[2]),
    ]
    for copy in mine:
        copy.start()
    exs = [sends(crossed, cross_ref.at[g], ex_send.at[d], ex_recv.at[d], at_x[d]) for d in range(1, NX)]
    eps = [sends(crossed, cross_ref.at[g], ep_send.at[0], ep_recv.at[0], pair)]
    for copy in exs + eps:
        copy.start()
    mine[0].wait()
    for copy in ys:
        copy.wait_recv()

    def ring(i, peer):
        o = owner_of(z, i - 2) if i > 2 else z
        return sends(rows_ref.at[o], rows_ref.at[o], ring_send.at[i], ring_recv.at[i], peer)

    def g_from(d):
        return lax.rem(x + NX - d, NX) * NCORE + c

    def across(i, d):
        o = owner_of(z, i)
        return sends(
            rows_ref.at[o, :, :, 0:PG], diag_ref.at[g, o], x_send.at[d, i], x_recv.at[d, i], at_x[d]
        )

    def to_pair(i, d):
        o = owner_of(z, i)
        if d == 0:
            return sends(
                rows_ref.at[o, :, :, 0:PG], diag_ref.at[g, o], pair_send.at[d, i], pair_recv.at[d, i], pair
            )
        gd = g_from(d)
        return sends(diag_ref.at[gd, o], diag_ref.at[gd, o], pair_send.at[d, i], pair_recv.at[d, i], pair)

    def keep(i):
        o = owner_of(z, i)
        return pltpu.make_async_copy(rows_ref.at[o, :, :, 0:PG], diag_ref.at[g, o], local.at[3 + i])

    def relay(i):
        for d in range(1, NX):
            across(i, d).wait_recv()
            to_pair(i, d).start()

    ring(1, up).start()
    ring(2, down).start()
    for i in range(NZ):
        if i > 0:
            ring(i, up if i % 2 == 1 else down).wait_recv()
            if i + 2 < NZ:
                ring(i + 2, up if i % 2 == 1 else down).start()
        for d in range(1, NX):
            across(i, d).start()
        to_pair(i, 0).start()
        keep(i).start()
        if i > 1:
            relay(i - 2)
    for d, copy in enumerate(exs, 1):
        copy.wait_recv()
        gd = g_from(d)
        eps.append(sends(cross_ref.at[gd], cross_ref.at[gd], ep_send.at[d], ep_recv.at[d], pair))
        eps[-1].start()
    relay(NZ - 2)
    relay(NZ - 1)

    for i in range(NZ):
        keep(i).wait()
        for d in range(NX):
            to_pair(i, d).wait_recv()
            to_pair(i, d).wait_send()
        for d in range(1, NX):
            across(i, d).wait_send()
        if i > 0:
            ring(i, up if i % 2 == 1 else down).wait_send()
    for copy in eps:
        copy.wait_recv()
        copy.wait_send()
    for copy in sums + ys + exs:
        copy.wait_send()
    mine[1].wait()
    mine[2].wait()


def spread(part, damp):
    vmem = pl.BlockSpec(memory_space=VMEM)
    return pl.pallas_call(
        spread_kernel,
        out_shape=(
            jax.ShapeDtypeStruct((LEFT, RIGHT), F32),
            jax.ShapeDtypeStruct((NZ, NY, PT, RIGHT), F32),
            jax.ShapeDtypeStruct((NG, NZ, NY, PT, PG), F32),
            jax.ShapeDtypeStruct((NG, COLS, PG), F32),
        ),
        in_specs=[vmem] * 2,
        out_specs=(vmem,) * 4,
        scratch_shapes=[VMEM((NY, LEFT, RIGHT), F32), VMEM((LEFT, RIGHT), F32)]
        + [DMA((NY,))] * 4
        + [DMA((NZ,))] * 2
        + [DMA((NX, NZ))] * 4
        + [DMA((NX,))] * 4
        + [DMA((3 + NZ,))],
        compiler_params=pltpu.CompilerParams(
            collective_id=1, has_side_effects=True, vmem_limit_bytes=40 << 20
        ),
        name="spread",
    )(part, damp)


def inverse_factor(m):
    lane = lax.broadcasted_iota(jnp.int32, (8, B), 1)
    sub = lax.broadcasted_iota(jnp.int32, (8, B), 0)
    tiles = [m[8 * i : 8 * i + 8, :] for i in range(B // 8)]
    full = lambda v: jnp.broadcast_to(v, (8, B))
    column = lambda t, j: jnp.take_along_axis(t, jnp.full((8, B), j, jnp.int32), axis=1)
    for j in range(0, B, 4):
        q, s = divmod(j, 8)
        t = tiles[q]
        cs = [column(t, j + p) for p in range(4)]
        here = (lane >= j) & (lane < j + 4)
        rows = []
        for p in range(4):
            row = jnp.where(here, 0.0, full(t[s + p : s + p + 1, :]))
            rows.append(jnp.where(lane == j + p, 1.0, row))
        low, root, solved = {}, [], []
        for p in range(4):
            pivot = full(cs[p][s + p : s + p + 1, :])
            for k in range(p):
                pivot = pivot - low[p, k] * low[p, k]
            root.append(lax.rsqrt(pivot))
            for i in range(p + 1, 4):
                v = full(cs[p][s + i : s + i + 1, :])
                for k in range(p):
                    v = v - low[i, k] * low[p, k]
                low[i, p] = v * root[p]
            v = rows[p]
            for k in range(p):
                v = v - low[p, k] * solved[k]
            solved.append(v * root[p])
        back = [None] * 4
        for p in reversed(range(4)):
            v = solved[p]
            for i in range(p + 1, 4):
                v = v - low[i, p] * back[i]
            back[p] = v * root[p]
        for i in range(q, B // 8):
            new = t if i == q else tiles[i]
            if i > q or s == 0:
                zs = [column(new, j + p) for p in range(4)]
                new = jnp.where(here, 0.0, new)
                for p in range(4):
                    new = new - zs[p] * back[p]
            if i == q:
                new = jnp.where(sub >= s + 4, new, t)
                for p in range(4):
                    new = jnp.where(sub == s + p, solved[p], new)
            tiles[i] = new
    w = jnp.concatenate(tiles, axis=0)
    r = lax.broadcasted_iota(jnp.int32, (B, B), 0)
    c = lax.broadcasted_iota(jnp.int32, (B, B), 1)
    return jnp.where(r >= c, w, 0.0)


GC = RIGHT - PG
WIDE = PICKED + GC + B


def solve_kernel(own_ref, rows_ref, diag_ref, cross_ref, trail_ref, factor_ref, acc, high, low):
    def block(k, carry):
        at = pl.ds(pl.multiple_of(k * B, B), B)
        for g in range(NG):
            acc[:, g * B : (g + 1) * B] = diag_ref[g, at, :]
        acc[:, PICKED : PICKED + GC] = rows_ref[at, PG:RIGHT]
        padded = jnp.concatenate([cross_ref[k], jnp.zeros((B - COLS, B), F32)], axis=0)
        acc[:, PICKED + GC :] = padded.T

        def before(j, carry):
            prior = pl.ds(pl.multiple_of(j * B, B), B)
            lh, ll = high[prior, at], low[prior, at]
            rh, rl = high[prior, :], low[prior, :]
            acc[...] -= dot(lh, rh, 0, 0) + (dot(lh, rl, 0, 0) + dot(ll, rh, 0, 0))
            return carry

        lax.fori_loop(0, k, before, 0)
        wh, wl = split(inverse_factor(acc[:, at]))
        ah, al = split(acc[...])
        u = dot(wh, ah, 1, 0) + (dot(wh, al, 1, 0) + dot(wl, ah, 1, 0))
        uh, ul = split(u)
        high[at, :] = uh
        low[at, :] = ul
        factor_ref[:, at] = u[:, PICKED : PICKED + GC].T[0:ROWS, :]
        return carry

    lax.fori_loop(0, NG, block, 0)
    gh, gl = high[:, PICKED : PICKED + GC], low[:, PICKED : PICKED + GC]
    th, tl = high[:, PICKED + GC :], low[:, PICKED + GC :]
    drop = dot(gh, th, 0, 0) + (dot(gh, tl, 0, 0) + dot(gl, th, 0, 0))
    gram = jnp.concatenate([own_ref[0:COLS, PG:RIGHT], jnp.zeros((B - COLS, GC), F32)], axis=0)
    trail_ref[...] = (gram.T - drop)[0:ROWS, 0:COLS]


def solve(own, rows, diag, cross):
    vmem = pl.BlockSpec(memory_space=VMEM)
    return pl.pallas_call(
        solve_kernel,
        out_shape=(
            jax.ShapeDtypeStruct((ROWS, COLS), F32),
            jax.ShapeDtypeStruct((ROWS, PICKED), F32),
        ),
        in_specs=[vmem] * 4,
        out_specs=(vmem, vmem),
        scratch_shapes=[VMEM((B, WIDE), F32), VMEM((PICKED, WIDE), BF16), VMEM((PICKED, WIDE), BF16)],
        compiler_params=pltpu.CompilerParams(vmem_limit_bytes=40 << 20),
        name="solve",
    )(own, rows, diag, cross)


def shards(
    tx_fields, rx_fields, layer_of_cell, layer_cond, tx_of_row, rx_of_row, damping, panel_order
):
    g = lax.axis_index("grp")
    t = lax.axis_index("tile")
    z, y = t // NY, t % NY
    levels = jnp.arange(layer_cond.shape[0], dtype=jnp.int32)
    hit = levels[:, None] == layer_of_cell[None, :]
    cond = jnp.sum(jnp.where(hit, layer_cond[:, None], 0.0), axis=0, keepdims=True)
    fields = jnp.concatenate([tx_fields, rx_fields], axis=0).reshape(2, 96, CELLS)

    pair_of_row = tx_of_row * 128 + rx_of_row
    picks = jnp.concatenate(
        [
            lax.dynamic_slice_in_dim(panel_order, g * PG, PG),
            lax.dynamic_slice_in_dim(panel_order, z * (PT * NY), PT * NY),
        ]
    )
    chosen = picks[:, None] == jnp.arange(M, dtype=jnp.int32)[None, :]
    pair_picks = jnp.sum(jnp.where(chosen, pair_of_row[None, :], 0), axis=1)
    damp_picks = jnp.sum(jnp.where(chosen, damping[None, :], 0.0), axis=1)
    right = [
        pair_picks[:PG],
        lax.dynamic_slice_in_dim(pair_of_row, g * ROWS, ROWS),
        jnp.full((RIGHT - PG - ROWS,), -1, jnp.int32),
    ]
    near = lax.dynamic_slice_in_dim(pair_of_row, z * (COLS * NY), COLS * NY).reshape(NY, COLS)
    left = jnp.concatenate([near, pair_picks[PG:].reshape(NY, PT)], axis=1).reshape(-1)
    pairs = jnp.concatenate(right + [left])[:, None]
    tx_hot = (pairs // 128 == jnp.arange(64)[None, :]).astype(BF16)
    rx_hot = ((pairs % 128 == jnp.arange(128)[None, :]) & (pairs >= 0)).astype(BF16)

    left_ids = jnp.concatenate(
        [t * COLS + jnp.arange(COLS), lax.dynamic_slice_in_dim(picks, PG + y * PT, PT)]
    )
    right_ids = jnp.concatenate(
        [picks[:PG], g * ROWS + jnp.arange(ROWS), jnp.full((RIGHT - PG - ROWS,), -1)]
    )
    left_damp = jnp.concatenate(
        [
            lax.dynamic_slice_in_dim(damping, t * COLS, COLS),
            lax.dynamic_slice_in_dim(damp_picks, PG + y * PT, PT),
        ]
    )
    damp = jnp.where(left_ids[:, None] == right_ids[None, :], left_damp[:, None], 0.0)

    part = gram_sums(fields, cond, tx_hot, rx_hot)
    own, rows, diag, cross = spread(part.reshape(NY, LEFT, RIGHT), damp)
    return solve(
        own, rows.reshape(PICKED, RIGHT), diag.reshape(NG, PICKED, PG), cross
    )


def solution(mesh):
    placed = (P(None, "tile"), P(None, "tile"), P("tile"), P(), P(), P(), P(), P())
    return jax.shard_map(
        shards,
        mesh=mesh,
        in_specs=placed,
        out_specs=(P("grp", "tile"), P("grp", None)),
        check_vma=False,
    )
```

time: 1150 us -> 169 us (0.15)
  waiting for transfers between devices: 812 us -> 0 us
  other arithmetic: 243 us -> 5.38 us
  Pallas kernels: 0 us -> 157 us
  matrix products: 35.7 us -> 0 us
  local copies, waits for them, and re-layouts: 28.4 us -> 2.9 us
  between operations: 20.2 us -> 0.73 us
    psum x6 -> x0, waiting for transfers between devices: 557 us -> none  [the longest x2 297 us: shards(): columns = lax.psum(jnp.dot(trailing, col_pick, precision=highest), 'tile')]
    another operation x37 -> x0, other arithmetic: 238 us -> none  [the longest x30 158 us: shards(): block_factor = jnp.linalg.cholesky(diag_block)]
    unnamed x9 -> x0, waiting for transfers between devices: 211 us -> none
    pallas_call x0 -> x3, Pallas kernels: none -> 157 us  [the longest x1 64.1 us: solve(): pl.pallas_call(solve_kernel, out_shape=(jax.ShapeDtypeStruct((ROWS, COLS)...]
    all_gather x1 -> x0, waiting for transfers between devices: 44.1 us -> none  [shards(): lax.all_gather(sens_own, 'grp', axis=0, tiled=True)]
    dot_general x8 -> x0, matrix products: 22.3 us -> none  [the longest x1 8.04 us: shards(): lax.dot_general(lax.all_gather(sens_own, 'grp', axis=0, tiled=True), sens...]
    another operation x35 -> x0, local copies, waits for them, and re-layouts: 16.7 us -> none  [the longest x27 16.4 us: shards(): lax.linalg.triangular_solve(block_factor, columns, left_side=False, lower...]
    another operation x26 -> x0, matrix products: 13.4 us -> none  [the longest x12 7.34 us: shards(): block_factor = jnp.linalg.cholesky(diag_block)]
  transfers between devices with their start and end apart: 8 -> 0, of which waited for: 8 -> 0; matrix products, arithmetic and copies ran while one was open for 0% -> 0% of each run, Pallas kernels for 0% -> 0%
where the time goes in v1:
time: 169 us; the launch traced here: 166 us
  Pallas kernels  157 us (93%)
  other arithmetic  5.38 us (3%)
  local copies, waits for them, and re-layouts  2.9 us (2%)
    pallas_call x1, Pallas kernels, solve(): pl.pallas_call(solve_kernel, out_shape=(jax.ShapeDtypeStruct((ROWS, COLS)...  64.1 us
    pallas_call x1, Pallas kernels, spread(): pl.pallas_call(spread_kernel, out_shape=(jax.ShapeDtypeStruct((LEFT, RIGH...  57.9 us
    pallas_call x1, Pallas kernels, gram_sums(): pl.pallas_call(gram_kernel, out_shape=jax.ShapeDtypeStruct((NY * LEFT, RI...  34.5 us

profile of v1, /device:TPU:16, one launch (start us, length us, event | category | flops | bytes accessed | tf_op | source)
XLA Modules:
  0.0 165.6 jit_solution(17300998215125788354)
XLA Ops:
  0.7 0.8 dynamic_slice.26
  1.5 0.8 fusion.6
  2.3 0.1 dynamic_slice.25
  2.4 0.1 pad_add_fusion.4
  2.5 1.2 select_reduce_fusion
  3.8 0.1 pad_maximum_fusion.1
  3.8 0.1 pad_add_fusion.2
  3.9 0.8 select_reduce_fusion.2
  4.7 0.7 multiply_add_fusion
  5.4 0.5 select_reduce_fusion.1
  6.0 0.1 fusion.5
  6.0 0.1 reshape.275
  6.1 0.1 reshape.276
  6.3 0.1 concatenate.56
  6.4 0.1 broadcast_compare_fusion
  6.5 0.1 add_select_fusion
  6.5 0.1 compare_select_fusion.damp_ref
  6.7 0.3 fusion.2.rx_hot_ref
  7.0 0.2 fusion.tx_hot_ref
  7.2 1.0 pad_maximum_fusion
  8.2 34.5 %gram_sums.1 = f32[480,512]{1,0:T(8,128)S(1)} custom-call(bf16[2,96,1024]{2,1,0:T(8,128)(2,1)S(1)} %bitcast.8, f32[1,1024]{1,0:T(1,128)S(1)} %bitcast.9, bf16[992,64]{1,0:T(8,128)(2,1)S(1)} %fusion.tx_hot_ref, bf16[992,128]{1,0:T(8,128)(2,1)S(1)} %fusion.2.rx_hot_ref), custom_call_target="tpu_custom_call" | custom-call | tf_op jit(solution)/shard_map/gram_sums/pallas_call | solution.py:165
  42.7 57.9 %spread.1 = (f32[120,512]{1,0:T(8,128)S(1)}, f32[8,4,32,512]{3,2,1,0:T(8,128)S(1)}, f32[8,8,4,32,128]{4,3,2,1,0:T(8,128)S(1)}, f32[8,88,128]{2,1,0:T(8,128)S(1)}) custom-call(f32[4,120,512]{2,1,0:T(8,128)S(1)} %bitcast.6, f32[120,512]{1,0:T(8,128)S(1)} %compare_select_fusion.damp_ref), custom_call_target="tpu_custom_call" | custom-call | tf_op jit(solution)/shard_map/spread/pallas_call | solution.py:300
  100.7 64.1 %solve.1 = (f32[352,88]{1,0:T(8,128)S(1)}, f32[352,1024]{1,0:T(8,128)}) custom-call(f32[120,512]{1,0:T(8,128)S(1)} %get-tuple-element.6.own_ref, f32[1024,512]{1,0:T(8,128)S(1)} %bitcast.7, f32[8,1024,128]{2,1,0:T(8,128)S(1)} %bitcast.5, f32[8,88,128]{2,1,0:T(8,128)S(1)} %get-tuple-element.9.cross_ref), custom_call_target="tpu_custom_call" | custom-call | tf_op jit(solution)/shard_map/solve/pallas_call | solution.py:417
  164.8 0.8 copy.11
  (7 shorter events, 0.2 us)

commit v2 on v1

v2 whole, which is shorter than its diff:
```python
import functools

import jax
import jax.numpy as jnp
from jax import lax
from jax.experimental import pallas as pl
from jax.experimental.pallas import tpu as pltpu
from jax.sharding import PartitionSpec as P

F32 = jnp.float32
BF16 = jnp.bfloat16
MESH = pl.DeviceIdType.MESH
VMEM = pltpu.VMEM
DMA = pltpu.SemaphoreType.DMA

M = 2816
NCELLS = 32768
PICKED = 1024
NX, NY, NZ, NCORE = 4, 4, 8, 2
NG = NX * NCORE
NT = NY * NZ
ROWS = M // NG
COLS = M // NT
PG = PICKED // NG
PT = PICKED // NT
CELLS = NCELLS // NT
RIGHT = 512
LEFT = COLS + PT
B = 128


def dot(a, b, ca, cb):
    return lax.dot_general(a, b, (((ca,), (cb,)), ((), ())), preferred_element_type=F32)


def split(x):
    hi = x.astype(BF16)
    return hi, (x - hi.astype(F32)).astype(BF16)


def places():
    g = lax.axis_index("grp")
    t = lax.axis_index("tile")
    return g // NCORE, g % NCORE, t // NY, t % NY


def at_z(z, y):
    return {"tile": lax.rem(z + NZ, NZ) * NY + y}


def greet(peers):
    barrier = pltpu.get_barrier_semaphore()
    for peer in peers:
        pl.semaphore_signal(barrier, inc=1, device_id=peer, device_id_type=MESH)
    pl.semaphore_wait(barrier, len(peers))


def sends(src, dst, send, recv, peer):
    return pltpu.make_async_remote_copy(
        src_ref=src, dst_ref=dst, send_sem=send, recv_sem=recv, device_id=peer, device_id_type=MESH
    )


def owner_of(z, i):
    hops = (i + 1) // 2
    return lax.rem(z + NZ + jnp.where(i % 2 == 1, -hops, hops), NZ)


def gram_kernel(
    fields_ref, cond_ref, tx_hot_ref, rx_hot_ref, out_ref, held, conds, sens,
    ring_send, ring_recv, cond_send, cond_recv, pair_send, pair_recv, local,
):
    x, c, z, y = places()
    up, down, pair = at_z(z + 1, y), at_z(z + NZ - 1, y), {"grp": x * NCORE + 1 - c}
    greet((up, down, pair))

    def ring(i, peer, first):
        o = z if first else owner_of(z, i - 2)
        half = fields_ref.at[c] if first else held.at[o, c]
        line = cond_ref if first else conds.at[o]
        return (
            sends(half, held.at[o, c], ring_send.at[i], ring_recv.at[i], peer),
            sends(line, conds.at[o], cond_send.at[i], cond_recv.at[i], peer),
        )

    def to_pair(i):
        o = owner_of(z, i)
        return sends(held.at[o, c], held.at[o, c], pair_send.at[i], pair_recv.at[i], pair)

    def start(copies):
        for copy in copies:
            copy.start()

    start(ring(1, up, True))
    start(ring(2, down, True))
    mine = pltpu.make_async_copy(fields_ref, held.at[z], local.at[0])
    mine_line = pltpu.make_async_copy(cond_ref, conds.at[z], local.at[1])
    mine.start()
    mine_line.start()
    out_ref[...] = jnp.zeros_like(out_ref)
    mine.wait()
    mine_line.wait()

    def arrive(i, peer, onward):
        for copy in ring(i, peer, False):
            copy.wait_recv()
        to_pair(i).start()
        if onward is not None:
            start(ring(i + 2, onward, False))

    def body(i, carry):
        @pl.when((i % 2 == 1) & (i < 6))
        def _():
            for copy in ring(i + 2, up, False):
                copy.wait_recv()
            to_pair(i + 2).start()

        @pl.when((i % 2 == 1) & (i < 4))
        def _():
            start(ring(i + 4, up, False))

        @pl.when((i % 2 == 0) & (i < 6))
        def _():
            for copy in ring(i + 2, down, False):
                copy.wait_recv()
            to_pair(i + 2).start()

        @pl.when((i % 2 == 0) & (i < 4))
        def _():
            start(ring(i + 4, down, False))

        @pl.when(i >= 1)
        def _():
            to_pair(i).wait_recv()

        o = owner_of(z, i)
        width = 256

        def chunk(j, carry):
            at = pl.ds(pl.multiple_of(j * width, width), width)
            txs = held[o, 0, 0:64, at]
            rxs = jnp.concatenate([held[o, 0, 64:96, at], held[o, 1, :, at]], axis=0)
            part = dot(tx_hot_ref[...], txs, 1, 0) * dot(rx_hot_ref[...], rxs, 1, 0)
            sens[:, at] = (part * conds[o, :, at]).astype(BF16)
            return carry

        lax.fori_loop(0, CELLS // width, chunk, 0)
        out_ref[...] += dot(sens[RIGHT:, :], sens[0:RIGHT, :], 1, 1)
        return carry

    for copy in ring(1, up, True):
        copy.wait_recv()
    to_pair(1).start()
    start(ring(3, up, False))
    lax.fori_loop(0, NZ, body, 0)

    for i in range(1, NZ):
        for copy in ring(i, up if i % 2 == 1 else down, i < 3):
            copy.wait_send()
        to_pair(i).wait_send()


def gram_sums(fields, cond, tx_hot, rx_hot):
    vmem = pl.BlockSpec(memory_space=VMEM)
    return pl.pallas_call(
        gram_kernel,
        out_shape=jax.ShapeDtypeStruct((NY * LEFT, RIGHT), F32),
        in_specs=[vmem] * 4,
        out_specs=vmem,
        scratch_shapes=[
            VMEM((NZ, NCORE, 96, CELLS), BF16),
            VMEM((NZ, 1, CELLS), F32),
            VMEM((RIGHT + NY * LEFT, CELLS), BF16),
        ]
        + [DMA((NZ,))] * 6
        + [DMA((2,))],
        compiler_params=pltpu.CompilerParams(
            collective_id=0, has_side_effects=True, vmem_limit_bytes=40 << 20
        ),
        name="gram_sums",
    )(fields, cond, tx_hot, rx_hot)


def tree(vs):
    while len(vs) > 1:
        vs = [vs[i] + vs[i + 1] if i + 1 < len(vs) else vs[i] for i in range(0, len(vs), 2)]
    return vs[0]


def inverse_factor(m):
    W = 16
    H = W // 8
    lane = lax.broadcasted_iota(jnp.int32, (8, B), 1)
    sub = lax.broadcasted_iota(jnp.int32, (8, B), 0)
    tiles = [m[8 * i : 8 * i + 8, :] for i in range(B // 8)]
    full = lambda v: jnp.broadcast_to(v, (8, B))
    column = lambda t, j: jnp.take_along_axis(t, jnp.full((8, B), j, jnp.int32), axis=1)
    for j in range(0, B, W):
        q = j // 8
        here = (lane >= j) & (lane < j + W)
        cs = {}
        for p in range(W):
            for h in range(p // 8, H):
                cs[p, h] = column(tiles[q + h], j + p)
        rows = [
            jnp.where(lane == j + 8 * h + sub, 1.0, jnp.where(here, 0.0, tiles[q + h])) for h in range(H)
        ]
        pivots, inverses, solved, low = [], [], [], {}
        for p in range(W):
            hp, s = divmod(p, 8)
            pivot = full(cs[p, hp][s : s + 1, :])
            inverse = 1.0 / pivot
            pivots.append(pivot)
            inverses.append(inverse)
            row = full(rows[hp][s : s + 1, :])
            solved.append(row)
            for k in range(p + 1, W):
                low[k, p] = full(cs[p, k // 8][k % 8 : k % 8 + 1, :]) * inverse
                for h in range(k // 8, H):
                    cs[k, h] = cs[k, h] - cs[p, h] * low[k, p]
            scaled = row * inverse
            for h in range(hp, H):
                if h == hp and s == 7:
                    continue
                f = jnp.where(sub > s, cs[p, h], 0.0) if h == hp else cs[p, h]
                rows[h] = rows[h] - f * scaled
        back = [None] * W
        for p in reversed(range(W)):
            v = solved[p] * inverses[p]
            for i in reversed(range(p + 1, W)):
                v = v - low[i, p] * back[i]
            back[p] = v
        for i in range(q + H, B // 8):
            terms = [column(tiles[i], j + p) * back[p] for p in range(W)]
            tiles[i] = jnp.where(here, 0.0, tiles[i]) - tree(terms)
        for h in range(H):
            scale = pivots[8 * h]
            for s in range(1, 8):
                scale = jnp.where(sub == s, pivots[8 * h + s], scale)
            tiles[q + h] = rows[h] * lax.rsqrt(scale)
    w = jnp.concatenate(tiles, axis=0)
    r = lax.broadcasted_iota(jnp.int32, (B, B), 0)
    c = lax.broadcasted_iota(jnp.int32, (B, B), 1)
    return jnp.where(r >= c, w, 0.0)


GC = RIGHT - PG
SIDE = GC + B


def dot3(ah, al, bh, bl, ca, cb):
    return dot(ah, bh, ca, cb) + (dot(ah, bl, ca, cb) + dot(al, bh, ca, cb))


def block_of(k):
    return pl.ds(pl.multiple_of(k * B, B), B)


DIAG, PICK, CROSS, REST = 0, 1, 2, 3
PARTS = (
    (slice(COLS, LEFT), slice(0, PG)),
    (slice(COLS, LEFT), slice(PG, RIGHT)),
    (slice(0, COLS), slice(0, PG)),
    (slice(0, COLS), slice(PG, RIGHT)),
)


def solve_kernel(
    part_ref, damp_ref, trail_ref, factor_ref,
    now, acc, nxt, high, low, wh, wl, xh, xl, got, diag, side_rows, cross, rest,
    rs_send, rs_recv, dz_send, dz_recv, dy_send, dy_recv, dx_send, dx_recv, dp_send, dp_recv,
    cz_send, cz_recv, cy_send, cy_recv, ex_send, ex_recv, ep_send, ep_recv,
):
    x, c, z, y = places()
    g = x * NCORE + c
    pair = {"grp": x * NCORE + 1 - c}
    at_y = [None] + [{"tile": z * NY + lax.rem(y + d, NY)} for d in range(1, NY)]
    at_x = [None] + [{"grp": lax.rem(x + d, NX) * NCORE + c} for d in range(1, NX)]
    in_z = [None] + [{"tile": lax.rem(z + d, NZ) * NY + y} for d in range(1, NZ)]
    greet(at_y[1:] + at_x[1:] + in_z[1:] + [pair])

    def rs(p, d):
        rows, cols = PARTS[p]
        return sends(
            part_ref.at[lax.rem(y + d, NY), rows, cols], got.at[d - 1, rows, cols],
            rs_send.at[p, d], rs_recv.at[p, d], at_y[d],
        )

    def start_sums(p):
        for d in range(1, NY):
            rs(p, d).start()

    def summed(p):
        rows, cols = PARTS[p]
        total = part_ref[y, rows, cols]
        for d in range(1, NY):
            rs(p, d).wait_recv()
            total += got[d - 1, rows, cols]
        return total * (1.0 / NCELLS) + damp_ref[rows, cols]

    def dz(d):
        return sends(diag.at[g, z, y], diag.at[g, z, y], dz_send.at[d], dz_recv.at[d], in_z[d])

    def dy(zz, d):
        return sends(diag.at[g, zz, y], diag.at[g, zz, y], dy_send.at[zz, d], dy_recv.at[zz, d], at_y[d])

    def dx(zz, d):
        return sends(diag.at[g, zz], diag.at[g, zz], dx_send.at[zz, d], dx_recv.at[zz, d], at_x[d])

    def dp(zz, d):
        gd = lax.rem(x + NX - d, NX) * NCORE + c
        return sends(diag.at[gd, zz], diag.at[gd, zz], dp_send.at[zz, d], dp_recv.at[zz, d], pair)

    def cz(d):
        return sends(side_rows.at[z, y], side_rows.at[z, y], cz_send.at[d], cz_recv.at[d], in_z[d])

    def cy(zz, d):
        return sends(side_rows.at[zz, y], side_rows.at[zz, y], cy_send.at[zz, d], cy_recv.at[zz, d], at_y[d])

    def ex(d):
        return sends(cross.at[g], cross.at[g], ex_send.at[d], ex_recv.at[d], at_x[d])

    def ep(d):
        gd = lax.rem(x + NX - d, NX) * NCORE + c
        return sends(cross.at[gd], cross.at[gd], ep_send.at[d], ep_recv.at[d], pair)

    def arrived(zz, copy, sem_recv, ref):
        d = lax.rem(z + NZ - zz, NZ)

        @pl.when(d != 0)
        def _():
            sends(ref.at[zz, y], ref.at[zz, y], sem_recv.at[d], sem_recv.at[d], pair).wait_recv()

    def across(zz):
        for d in range(1, NX):
            dx(zz, d).wait_recv()
            dp(zz, d).start()

    def complete(zz):
        for d in range(NX):
            dp(zz, d).wait_recv()

    start_sums(DIAG)
    high[...] = jnp.zeros_like(high)
    low[...] = jnp.zeros_like(low)
    xh[...] = jnp.zeros_like(xh)
    xl[...] = jnp.zeros_like(xl)
    acc[...] = jnp.zeros_like(acc)
    wh[0] = jnp.zeros((B, B), BF16)
    wl[0] = jnp.zeros((B, B), BF16)
    diag[g, z, y] = summed(DIAG)
    for d in range(1, NZ):
        dz(d).start()
    start_sums(PICK)
    for zz in range(NZ):
        arrived(zz, None, dz_recv, diag.at[g])
        for d in range(1, NY):
            dy(zz, d).start()
    start_sums(CROSS)
    for zz in range(NZ):
        for d in range(1, NY):
            dy(zz, d).wait_recv()
        for d in range(1, NX):
            dx(zz, d).start()
        dp(zz, 0).start()
    start_sums(REST)
    across(0)
    across(1)
    complete(0)

    def diag_rows(k, begin):
        return jnp.concatenate([diag[i, k].reshape(B, B) for i in range(begin, NG)], axis=1)

    nxt[...] = diag_rows(0, 0)
    now[...] = diag[0, 0].reshape(B, B)

    def block(k, begin, depth):
        w = inverse_factor(now[...])
        last = jnp.maximum(k - 1, 0)
        cols = slice(begin * B, PICKED)
        ah, al = split(acc[:, cols])
        uh, ul = split(dot3(wh[last], wl[last], ah, al, 1, 0))
        high[block_of(last), cols] = uh
        low[block_of(last), cols] = ul
        at = block_of(k)
        acc[:, cols] = nxt[:, cols] - dot3(high[block_of(last), at], low[block_of(last), at], uh, ul, 0, 0)
        after = jnp.minimum(k + 1, NG - 1)
        there = block_of(after)
        nxt[:, cols] = diag_rows(after, begin) - dot3(
            high[0:depth, there], low[0:depth, there], high[0:depth, cols], low[0:depth, cols], 0, 0
        )
        nh, nl = split(w)
        wh[k] = nh
        wl[k] = nl
        bh, bl = split(acc[:, there])
        vh, vl = split(dot3(nh, nl, bh, bl, 1, 0))
        now[...] = nxt[:, there] - dot3(vh, vl, vh, vl, 0, 0)

    def side(i, depth):
        at = block_of(i)
        padded = jnp.concatenate([cross[i], jnp.zeros((B - COLS, B), F32)], axis=0).T
        start = jnp.concatenate([side_rows[i].reshape(B, GC), padded], axis=1)
        done = dot3(high[0:depth, at], low[0:depth, at], xh[0:depth, :], xl[0:depth, :], 0, 0)
        sh, sl = split(start - done)
        u = dot3(wh[i], wl[i], sh, sl, 1, 0)
        uh, ul = split(u)
        xh[at, :] = uh
        xl[at, :] = ul
        factor_ref[:, at] = u[:, 0:GC].T[0:ROWS, :]

    def first(k, carry):
        across(k + 2)
        complete(k + 1)

        @pl.when(k == 0)
        def _():
            side_rows[z, y] = summed(PICK)
            for d in range(1, NZ):
                cz(d).start()
            cross[g] = summed(CROSS)
            for d in range(1, NX):
                ex(d).start()
            ep(0).start()

        @pl.when(k == 2)
        def _():
            for zz in range(NZ):
                arrived(zz, None, cz_recv, side_rows)
                for d in range(1, NY):
                    cy(zz, d).start()
            for d in range(1, NX):
                ex(d).wait_recv()
                ep(d).start()

        block(k, 0, 4 * B)
        return carry

    def here(i):
        for d in range(1, NY):
            cy(i, d).wait_recv()

    def second(k, carry):
        across(k + 2)
        complete(k + 1)
        i = 2 * (k - 4)
        here(i)
        here(i + 1)
        block(k, 3, 5 * B)
        side(i, 4 * B)
        side(i + 1, 4 * B)
        return carry

    def third(k, carry):
        @pl.when(k < NG - 1)
        def _():
            complete(k + 1)

        here(k - 2)
        block(k, 5, 7 * B)
        side(k - 2, 6 * B)
        return carry

    lax.fori_loop(0, 4, first, 0)
    for d in range(NX):
        ep(d).wait_recv()
    lax.fori_loop(4, 6, second, 0)
    lax.fori_loop(6, NG, third, 0)
    here(NG - 2)
    here(NG - 1)
    side(NG - 2, 6 * B)
    side(NG - 1, 7 * B)
    rest[0:COLS, :] = summed(REST)
    rest[COLS:, :] = jnp.zeros((B - COLS, GC), F32)
    drop = dot3(xh[:, 0:GC], xl[:, 0:GC], xh[:, GC:], xl[:, GC:], 0, 0)
    trail_ref[...] = (rest[...].T - drop)[0:ROWS, 0:COLS]

    for d in range(1, NY):
        for p in range(4):
            rs(p, d).wait_send()
        for zz in range(NZ):
            dy(zz, d).wait_send()
            cy(zz, d).wait_send()
    for d in range(1, NZ):
        dz(d).wait_send()
        cz(d).wait_send()
    for d in range(NX):
        for zz in range(NZ):
            if d:
                dx(zz, d).wait_send()
            dp(zz, d).wait_send()
        if d:
            ex(d).wait_send()
        ep(d).wait_send()


def solve(part, damp):
    vmem = pl.BlockSpec(memory_space=VMEM)
    return pl.pallas_call(
        solve_kernel,
        out_shape=(
            jax.ShapeDtypeStruct((ROWS, COLS), F32),
            jax.ShapeDtypeStruct((ROWS, PICKED), F32),
        ),
        in_specs=[vmem] * 2,
        out_specs=(vmem, vmem),
        scratch_shapes=[
            VMEM((B, B), F32),
            VMEM((B, PICKED), F32),
            VMEM((B, PICKED), F32),
            VMEM((PICKED, PICKED), BF16),
            VMEM((PICKED, PICKED), BF16),
            VMEM((NG, B, B), BF16),
            VMEM((NG, B, B), BF16),
            VMEM((PICKED, SIDE), BF16),
            VMEM((PICKED, SIDE), BF16),
            VMEM((NY - 1, LEFT, RIGHT), F32),
            VMEM((NG, NZ, NY, PT, PG), F32),
            VMEM((NZ, NY, PT, GC), F32),
            VMEM((NG, COLS, PG), F32),
            VMEM((B, GC), F32),
        ]
        + [DMA((4, NY))] * 2
        + [DMA((NZ,))] * 2
        + [DMA((NZ, NY))] * 2
        + [DMA((NZ, NX))] * 4
        + [DMA((NZ,))] * 2
        + [DMA((NZ, NY))] * 2
        + [DMA((NX,))] * 4,
        compiler_params=pltpu.CompilerParams(
            collective_id=1, has_side_effects=True, vmem_limit_bytes=48 << 20
        ),
        name="solve",
    )(part, damp)


def shards(
    tx_fields, rx_fields, layer_of_cell, layer_cond, tx_of_row, rx_of_row, damping, panel_order
):
    g = lax.axis_index("grp")
    t = lax.axis_index("tile")
    z, y = t // NY, t % NY
    levels = jnp.arange(layer_cond.shape[0], dtype=jnp.int32)
    hit = levels[:, None] == layer_of_cell[None, :]
    cond = jnp.sum(jnp.where(hit, layer_cond[:, None], 0.0), axis=0, keepdims=True)
    fields = jnp.concatenate([tx_fields, rx_fields], axis=0).reshape(2, 96, CELLS)

    pair_of_row = tx_of_row * 128 + rx_of_row
    picks = jnp.concatenate(
        [
            lax.dynamic_slice_in_dim(panel_order, g * PG, PG),
            lax.dynamic_slice_in_dim(panel_order, z * (PT * NY), PT * NY),
        ]
    )
    chosen = picks[:, None] == jnp.arange(M, dtype=jnp.int32)[None, :]
    pair_picks = jnp.sum(jnp.where(chosen, pair_of_row[None, :], 0), axis=1)
    damp_picks = jnp.sum(jnp.where(chosen, damping[None, :], 0.0), axis=1)
    right = [
        pair_picks[:PG],
        lax.dynamic_slice_in_dim(pair_of_row, g * ROWS, ROWS),
        jnp.full((RIGHT - PG - ROWS,), -1, jnp.int32),
    ]
    near = lax.dynamic_slice_in_dim(pair_of_row, z * (COLS * NY), COLS * NY).reshape(NY, COLS)
    left = jnp.concatenate([near, pair_picks[PG:].reshape(NY, PT)], axis=1).reshape(-1)
    pairs = jnp.concatenate(right + [left])[:, None]
    tx_hot = (pairs // 128 == jnp.arange(64)[None, :]).astype(BF16)
    rx_hot = ((pairs % 128 == jnp.arange(128)[None, :]) & (pairs >= 0)).astype(BF16)

    left_ids = jnp.concatenate(
        [t * COLS + jnp.arange(COLS), lax.dynamic_slice_in_dim(picks, PG + y * PT, PT)]
    )
    right_ids = jnp.concatenate(
        [picks[:PG], g * ROWS + jnp.arange(ROWS), jnp.full((RIGHT - PG - ROWS,), -1)]
    )
    left_damp = jnp.concatenate(
        [
            lax.dynamic_slice_in_dim(damping, t * COLS, COLS),
            lax.dynamic_slice_in_dim(damp_picks, PG + y * PT, PT),
        ]
    )
    damp = jnp.where(left_ids[:, None] == right_ids[None, :], left_damp[:, None], 0.0)

    part = gram_sums(fields, cond, tx_hot, rx_hot)
    return solve(part.reshape(NY, LEFT, RIGHT), damp)


def solution(mesh):
    placed = (P(None, "tile"), P(None, "tile"), P("tile"), P(), P(), P(), P(), P())
    return jax.shard_map(
        shards,
        mesh=mesh,
        in_specs=placed,
        out_specs=(P("grp", "tile"), P("grp", None)),
        check_vma=False,
    )
```

time: 169 us -> 120 us (0.71); the launches traced: 166 us -> 119 us
  Pallas kernels: 157 us -> 109 us
    pallas_call x1 -> x0, Pallas kernels: 57.9 us -> none  [spread(): pl.pallas_call(spread_kernel, out_shape=(jax.ShapeDtypeStruct((LEFT, RIGH...]
    pallas_call x1, Pallas kernels: 64.1 us -> 74.9 us  [solve(): pl.pallas_call(solve_kernel, out_shape=(jax.ShapeDtypeStruct((ROWS, COLS)...]
where the time goes in v2:
time: 120 us; the launch traced here: 119 us
  Pallas kernels  109 us (91%)
  other arithmetic  5.38 us (4%)
  local copies, waits for them, and re-layouts  4 us (3%)
    pallas_call x1, Pallas kernels, solve(): pl.pallas_call(solve_kernel, out_shape=(jax.ShapeDtypeStruct((ROWS, COLS)...  74.9 us
    pallas_call x1, Pallas kernels, gram_sums(): pl.pallas_call(gram_kernel, out_shape=jax.ShapeDtypeStruct((NY * LEFT, RI...  34.5 us

profile of v2, /device:TPU:16, one launch (start us, length us, event | category | flops | bytes accessed | tf_op | source)
XLA Modules:
  0.0 119.5 jit_solution(15029333145402935602)
XLA Ops:
  0.7 0.8 dynamic_slice.26
  1.5 0.8 fusion.6
  2.3 0.1 dynamic_slice.25
  2.4 0.1 pad_add_fusion.4
  2.5 1.2 %select_reduce_fusion = f32[256]{0:T(256)S(1)} fusion(f32[2816]{0:T(1024)} %param.14, s32[256]{0:T(256)S(1)} %pad_add_fusion.3), kind=kLoop, calls=%fused_computation | loop fusion | flops 2162432 | bytes 13312 | tf_op jit(solution)/shard_map/reduce_sum | solution.py:556
  3.8 0.1 pad_maximum_fusion.1
  3.8 0.1 pad_add_fusion.2
  3.9 0.8 select_reduce_fusion.2
  4.7 0.7 multiply_add_fusion
  5.4 0.5 select_reduce_fusion.1
  6.0 0.1 fusion.5
  6.0 0.1 reshape.269
  6.1 0.1 reshape.270
  6.3 0.1 concatenate.56
  6.4 0.1 broadcast_compare_fusion
  6.5 0.1 add_select_fusion
  6.5 0.1 compare_select_fusion.damp_ref
  6.7 0.3 fusion.2.rx_hot_ref
  7.0 0.2 fusion.tx_hot_ref
  7.2 1.0 pad_maximum_fusion
  8.2 34.5 %gram_sums.1 = f32[480,512]{1,0:T(8,128)S(1)} custom-call(bf16[2,96,1024]{2,1,0:T(8,128)(2,1)S(1)} %bitcast.4, f32[1,1024]{1,0:T(1,128)S(1)} %bitcast.5, bf16[992,64]{1,0:T(8,128)(2,1)S(1)} %fusion.tx_hot_ref, bf16[992,128]{1,0:T(8,128)(2,1)S(1)} %fusion.2.rx_hot_ref), custom_call_target="tpu_custom_call" | custom-call | tf_op jit(solution)/shard_map/gram_sums/pallas_call | solution.py:165
  42.7 74.9 %solve.1 = (f32[352,88]{1,0:T(8,128)S(1)}, f32[352,1024]{1,0:T(8,128)S(1)}) custom-call(f32[4,120,512]{2,1,0:T(8,128)S(1)} %bitcast.3, f32[120,512]{1,0:T(8,128)S(1)} %compare_select_fusion.damp_ref), custom_call_target="tpu_custom_call" | custom-call | tf_op jit(solution)/shard_map/solve/pallas_call | solution.py:498
  117.6 0.8 copy.11
  118.4 1.1 copy.13
  (7 shorter events, 0.2 us)

commit v3 on v2

--- a/solution.py
+++ b/solution.py
@@ -27,6 +27,7 @@
 RIGHT = 512
 LEFT = COLS + PT
 B = 128
+GC = RIGHT - PG
 
 
 def dot(a, b, ca, cb):
@@ -66,119 +67,164 @@
     return lax.rem(z + NZ + jnp.where(i % 2 == 1, -hops, hops), NZ)
 
 
-def gram_kernel(
-    fields_ref, cond_ref, tx_hot_ref, rx_hot_ref, out_ref, held, conds, sens,
+MSGS = 3
+ROW_STEP = 32
+
+
+def look_up(at, table):
+    lanes = lax.broadcasted_iota(jnp.int32, (at.shape[0], table.shape[1]), 1)
+    return jnp.sum(jnp.where(at == lanes, table, 0.0), axis=1, keepdims=True)
+
+
+def prepare(order_ref, tx_row_ref, rx_row_ref, damp_row_ref, tx_hot, rx_hot, damp, g, z, y, t):
+    order = order_ref[:, 0:PICKED].astype(F32)
+    txs, rxs = tx_row_ref[...].astype(F32), rx_row_ref[...].astype(F32)
+
+    def rows(i, carry):
+        begin = pl.multiple_of(i * ROW_STEP, ROW_STEP)
+        r = begin + lax.broadcasted_iota(jnp.int32, (ROW_STEP, 1), 0)
+        s = r - RIGHT
+        part = (s >= LEFT).astype(jnp.int32) + (s >= 2 * LEFT).astype(jnp.int32) + (s >= 3 * LEFT).astype(jnp.int32)
+        q = s - part * LEFT
+        right = s < 0
+        is_pick = (right & (r < PG)) | ((s >= 0) & (q >= COLS))
+        place = jnp.where(right, g * PG + r, (z * NY + part) * PT + q - COLS)
+        plain = jnp.where(right, g * ROWS + r - PG, (z * NY + part) * COLS + q)
+        plain = jnp.where(right & (r >= PG + ROWS), -1, plain)
+        picked = look_up(jnp.where(is_pick, place, -1), order).astype(jnp.int32)
+        ids = jnp.where(is_pick, picked, plain)
+        lanes = lax.broadcasted_iota(jnp.int32, (ROW_STEP, M), 1)
+        hit = ids == lanes
+        none = jnp.where(ids < 0, -1.0, 0.0)
+        txv = jnp.sum(jnp.where(hit, txs, 0.0), axis=1, keepdims=True) + none
+        rxv = jnp.sum(jnp.where(hit, rxs, 0.0), axis=1, keepdims=True) + none
+        here = pl.ds(begin, ROW_STEP)
+        lane = lax.broadcasted_iota(jnp.int32, (ROW_STEP, 128), 1).astype(F32)
+        tx_hot[here, :] = jnp.where(txv == lane, 1.0, 0.0).astype(BF16)
+        rx_hot[here, :] = jnp.where(rxv == lane, 1.0, 0.0).astype(BF16)
+        return carry
+
+    lax.fori_loop(0, (RIGHT + NY * LEFT) // ROW_STEP, rows, 0)
+
+    q = lax.broadcasted_iota(jnp.int32, (LEFT, 1), 0)
+    picked = look_up(jnp.where(q >= COLS, t * PT + q - COLS, -1), order).astype(jnp.int32)
+    left = jnp.where(q >= COLS, picked, t * COLS + q)
+    near = look_up(left, damp_row_ref[...])
+    natural = lax.broadcasted_iota(jnp.int32, (1, GC), 1)
+    natural = jnp.where(natural < ROWS, g * ROWS + natural, -1)
+    right = jnp.concatenate([order_ref[:, pl.ds(pl.multiple_of(g * PG, PG), PG)], natural], axis=1)
+    damp[...] = jnp.where(left == right, near, 0.0)
+
+
+def gram_part(
+    tx_ref, rx_ref, layer_ref, cond_ref, prep, part, held, conds, sens, tx_hot, rx_hot,
     ring_send, ring_recv, cond_send, cond_recv, pair_send, pair_recv, local,
 ):
     x, c, z, y = places()
     up, down, pair = at_z(z + 1, y), at_z(z + NZ - 1, y), {"grp": x * NCORE + 1 - c}
-    greet((up, down, pair))
-
-    def ring(i, peer, first):
-        o = z if first else owner_of(z, i - 2)
-        half = fields_ref.at[c] if first else held.at[o, c]
-        line = cond_ref if first else conds.at[o]
-        return (
-            sends(half, held.at[o, c], ring_send.at[i], ring_recv.at[i], peer),
-            sends(line, conds.at[o], cond_send.at[i], cond_recv.at[i], peer),
-        )
-
-    def to_pair(i):
+
+    def own(m):
+        if m == 0:
+            return tx_ref.at[pl.ds(pl.multiple_of(c * 32, 32), 32), :]
+        return rx_ref.at[pl.ds(pl.multiple_of(c * 64 + (m - 1) * 32, 32), 32), :]
+
+    def way(i, m):
+        return i % 2 == 1 if i < NZ - 1 else m == 0
+
+    def ring(i, m):
+        first = i < 3
+        rising = way(i, m)
+        prior = i - 2 if i < NZ - 1 or rising else i - 1
+        o = z if first else owner_of(z, prior)
+        src = own(m) if first else held.at[o, c, m]
+        return sends(src, held.at[o, c, m], ring_send.at[i, m], ring_recv.at[i, m], up if rising else down)
+
+    def line(i):
+        o = z if i < 3 else owner_of(z, i - 2)
+        return sends(conds.at[o], conds.at[o], cond_send.at[i], cond_recv.at[i], up if i % 2 == 1 else down)
+
+    def to_pair(i, m):
         o = owner_of(z, i)
-        return sends(held.at[o, c], held.at[o, c], pair_send.at[i], pair_recv.at[i], pair)
-
-    def start(copies):
-        for copy in copies:
-            copy.start()
-
-    start(ring(1, up, True))
-    start(ring(2, down, True))
-    mine = pltpu.make_async_copy(fields_ref, held.at[z], local.at[0])
-    mine_line = pltpu.make_async_copy(cond_ref, conds.at[z], local.at[1])
-    mine.start()
-    mine_line.start()
-    out_ref[...] = jnp.zeros_like(out_ref)
-    mine.wait()
-    mine_line.wait()
-
-    def arrive(i, peer, onward):
-        for copy in ring(i, peer, False):
-            copy.wait_recv()
-        to_pair(i).start()
-        if onward is not None:
-            start(ring(i + 2, onward, False))
+        return sends(held.at[o, c, m], held.at[o, c, m], pair_send.at[i, m], pair_recv.at[i, m], pair)
+
+    def arrive(i, m):
+        ring(i, m).wait_recv()
+        if i < NZ - 3:
+            ring(i + 2, m).start()
+        elif i < NZ - 1 and way(NZ - 1, m) == (i % 2 == 1):
+            ring(NZ - 1, m).start()
+        to_pair(i, m).start()
+        if m == 0:
+            line(i).wait_recv()
+            if i + 2 < NZ:
+                line(i + 2).start()
+
+    for m in range(MSGS):
+        ring(1, m).start()
+        ring(2, m).start()
+    mine = []
+    for core in range(NCORE):
+        mine.append(pltpu.make_async_copy(tx_ref.at[32 * core : 32 * core + 32, :], held.at[z, core, 0], local.at[core, 0]))
+        for m in (1, 2):
+            at = 64 * core + 32 * (m - 1)
+            mine.append(pltpu.make_async_copy(rx_ref.at[at : at + 32, :], held.at[z, core, m], local.at[core, m]))
+    for copy in mine:
+        copy.start()
+    layer = layer_ref[...]
+    cond = jnp.zeros((1, CELLS), F32)
+    for level in range(32):
+        cond = jnp.where(layer == level, cond_ref[level], cond)
+    conds[z] = cond
+    line(1).start()
+    line(2).start()
+    prep()
+    part[...] = jnp.zeros_like(part)
+    for copy in mine:
+        copy.wait()
+    for m in range(MSGS):
+        arrive(1, m)
 
     def body(i, carry):
-        @pl.when((i % 2 == 1) & (i < 6))
-        def _():
-            for copy in ring(i + 2, up, False):
-                copy.wait_recv()
-            to_pair(i + 2).start()
-
-        @pl.when((i % 2 == 1) & (i < 4))
-        def _():
-            start(ring(i + 4, up, False))
-
-        @pl.when((i % 2 == 0) & (i < 6))
-        def _():
-            for copy in ring(i + 2, down, False):
-                copy.wait_recv()
-            to_pair(i + 2).start()
-
-        @pl.when((i % 2 == 0) & (i < 4))
-        def _():
-            start(ring(i + 4, down, False))
-
-        @pl.when(i >= 1)
-        def _():
-            to_pair(i).wait_recv()
+        for n in range(NZ - 1):
+            @pl.when(i == n)
+            def _():
+                for m in range(MSGS):
+                    if n + 2 < NZ - 1:
+                        arrive(n + 2, m)
+                    elif way(NZ - 1, m) == (n % 2 == 1):
+                        arrive(NZ - 1, m)
+
+        for n in range(1, NZ):
+            @pl.when(i == n)
+            def _():
+                for m in range(MSGS):
+                    to_pair(n, m).wait_recv()
 
         o = owner_of(z, i)
         width = 256
 
         def chunk(j, carry):
             at = pl.ds(pl.multiple_of(j * width, width), width)
-            txs = held[o, 0, 0:64, at]
-            rxs = jnp.concatenate([held[o, 0, 64:96, at], held[o, 1, :, at]], axis=0)
-            part = dot(tx_hot_ref[...], txs, 1, 0) * dot(rx_hot_ref[...], rxs, 1, 0)
-            sens[:, at] = (part * conds[o, :, at]).astype(BF16)
+            txs = jnp.concatenate([held[o, k, 0, :, at] for k in range(NCORE)], axis=0)
+            rxs = jnp.concatenate([held[o, k, m, :, at] for k in range(NCORE) for m in (1, 2)], axis=0)
+            both = dot(tx_hot[:, 0:64], txs, 1, 0) * dot(rx_hot[...], rxs, 1, 0)
+            sens[:, at] = (both * conds[o, :, at]).astype(BF16)
             return carry
 
         lax.fori_loop(0, CELLS // width, chunk, 0)
-        out_ref[...] += dot(sens[RIGHT:, :], sens[0:RIGHT, :], 1, 1)
+        part[...] += dot(sens[RIGHT:, :], sens[0:RIGHT, :], 1, 1).reshape(NY, LEFT, RIGHT)
         return carry
 
-    for copy in ring(1, up, True):
-        copy.wait_recv()
-    to_pair(1).start()
-    start(ring(3, up, False))
     lax.fori_loop(0, NZ, body, 0)
 
-    for i in range(1, NZ):
-        for copy in ring(i, up if i % 2 == 1 else down, i < 3):
-            copy.wait_send()
-        to_pair(i).wait_send()
-
-
-def gram_sums(fields, cond, tx_hot, rx_hot):
-    vmem = pl.BlockSpec(memory_space=VMEM)
-    return pl.pallas_call(
-        gram_kernel,
-        out_shape=jax.ShapeDtypeStruct((NY * LEFT, RIGHT), F32),
-        in_specs=[vmem] * 4,
-        out_specs=vmem,
-        scratch_shapes=[
-            VMEM((NZ, NCORE, 96, CELLS), BF16),
-            VMEM((NZ, 1, CELLS), F32),
-            VMEM((RIGHT + NY * LEFT, CELLS), BF16),
-        ]
-        + [DMA((NZ,))] * 6
-        + [DMA((2,))],
-        compiler_params=pltpu.CompilerParams(
-            collective_id=0, has_side_effects=True, vmem_limit_bytes=40 << 20
-        ),
-        name="gram_sums",
-    )(fields, cond, tx_hot, rx_hot)
+    def finish():
+        for i in range(1, NZ):
+            for m in range(MSGS):
+                ring(i, m).wait_send()
+                to_pair(i, m).wait_send()
+            line(i).wait_send()
+
+    return finish
 
 
 def tree(vs):
@@ -244,7 +290,6 @@
     return jnp.where(r >= c, w, 0.0)
 
 
-GC = RIGHT - PG
 SIDE = GC + B
 
 
@@ -265,8 +310,11 @@
 )
 
 
-def solve_kernel(
-    part_ref, damp_ref, trail_ref, factor_ref,
+def step_kernel(
+    tx_ref, rx_ref, layer_ref, cond_ref, tx_row_ref, rx_row_ref, damp_row_ref, order_ref,
+    trail_ref, factor_ref,
+    part_ref, damp_ref, held, conds, sens, tx_hot, rx_hot,
+    gr_send, gr_recv, gc_send, gc_recv, gp_send, gp_recv, local,
     now, acc, nxt, high, low, wh, wl, xh, xl, got, diag, side_rows, cross, rest,
     rs_send, rs_recv, dz_send, dz_recv, dy_send, dy_recv, dx_send, dx_recv, dp_send, dp_recv,
     cz_send, cz_recv, cy_send, cy_recv, ex_send, ex_recv, ep_send, ep_recv,
@@ -278,6 +326,16 @@
     at_x = [None] + [{"grp": lax.rem(x + d, NX) * NCORE + c} for d in range(1, NX)]
     in_z = [None] + [{"tile": lax.rem(z + d, NZ) * NY + y} for d in range(1, NZ)]
     greet(at_y[1:] + at_x[1:] + in_z[1:] + [pair])
+
+    def prep():
+        prepare(
+            order_ref, tx_row_ref, rx_row_ref, damp_row_ref, tx_hot, rx_hot, damp_ref, g, z, y, z * NY + y
+        )
+
+    finish = gram_part(
+        tx_ref, rx_ref, layer_ref, cond_ref, prep, part_ref, held, conds, sens, tx_hot, rx_hot,
+        gr_send, gr_recv, gc_send, gc_recv, gp_send, gp_recv, local,
+    )
 
     def rs(p, d):
         rows, cols = PARTS[p]
@@ -474,6 +532,7 @@
     drop = dot3(xh[:, 0:GC], xl[:, 0:GC], xh[:, GC:], xl[:, GC:], 0, 0)
     trail_ref[...] = (rest[...].T - drop)[0:ROWS, 0:COLS]
 
+    finish()
     for d in range(1, NY):
         for p in range(4):
             rs(p, d).wait_send()
@@ -493,17 +552,33 @@
         ep(d).wait_send()
 
 
-def solve(part, damp):
+def shards(
+    tx_fields, rx_fields, layer_of_cell, layer_cond, tx_of_row, rx_of_row, damping, panel_order
+):
     vmem = pl.BlockSpec(memory_space=VMEM)
+    smem = pl.BlockSpec(memory_space=pltpu.SMEM)
     return pl.pallas_call(
-        solve_kernel,
+        step_kernel,
         out_shape=(
             jax.ShapeDtypeStruct((ROWS, COLS), F32),
             jax.ShapeDtypeStruct((ROWS, PICKED), F32),
         ),
-        in_specs=[vmem] * 2,
+        in_specs=[vmem, vmem, vmem, smem, vmem, vmem, vmem, vmem],
         out_specs=(vmem, vmem),
         scratch_shapes=[
+            VMEM((NY, LEFT, RIGHT), F32),
+            VMEM((LEFT, RIGHT), F32),
+            VMEM((NZ, NCORE, MSGS, 32, CELLS), BF16),
+            VMEM((NZ, 1, CELLS), F32),
+            VMEM((RIGHT + NY * LEFT, CELLS), BF16),
+            VMEM((RIGHT + NY * LEFT, 128), BF16),
+            VMEM((RIGHT + NY * LEFT, 128), BF16),
+        ]
+        + [DMA((NZ, MSGS))] * 2
+        + [DMA((NZ,))] * 2
+        + [DMA((NZ, MSGS))] * 2
+        + [DMA((NCORE, MSGS))]
+        + [
             VMEM((B, B), F32),
             VMEM((B, PICKED), F32),
             VMEM((B, PICKED), F32),
@@ -527,60 +602,13 @@
         + [DMA((NZ, NY))] * 2
         + [DMA((NX,))] * 4,
         compiler_params=pltpu.CompilerParams(
-            collective_id=1, has_side_effects=True, vmem_limit_bytes=48 << 20
+            collective_id=0, has_side_effects=True, vmem_limit_bytes=56 << 20
         ),
-        name="solve",
-    )(part, damp)
-
-
-def shards(
-    tx_fields, rx_fields, layer_of_cell, layer_cond, tx_of_row, rx_of_row, damping, panel_order
-):
-    g = lax.axis_index("grp")
-    t = lax.axis_index("tile")
-    z, y = t // NY, t % NY
-    levels = jnp.arange(layer_cond.shape[0], dtype=jnp.int32)
-    hit = levels[:, None] == layer_of_cell[None, :]
-    cond = jnp.sum(jnp.where(hit, layer_cond[:, None], 0.0), axis=0, keepdims=True)
-    fields = jnp.concatenate([tx_fields, rx_fields], axis=0).reshape(2, 96, CELLS)
-
-    pair_of_row = tx_of_row * 128 + rx_of_row
-    picks = jnp.concatenate(
-        [
-            lax.dynamic_slice_in_dim(panel_order, g * PG, PG),
-            lax.dynamic_slice_in_dim(panel_order, z * (PT * NY), PT * NY),
-        ]
+        name="step",
+    )(
+        tx_fields, rx_fields, layer_of_cell[None, :], layer_cond,
+        tx_of_row[None, :], rx_of_row[None, :], damping[None, :], panel_order[None, :],
     )
-    chosen = picks[:, None] == jnp.arange(M, dtype=jnp.int32)[None, :]
-    pair_picks = jnp.sum(jnp.where(chosen, pair_of_row[None, :], 0), axis=1)
-    damp_picks = jnp.sum(jnp.where(chosen, damping[None, :], 0.0), axis=1)
-    right = [
-        pair_picks[:PG],
-        lax.dynamic_slice_in_dim(pair_of_row, g * ROWS, ROWS),
-        jnp.full((RIGHT - PG - ROWS,), -1, jnp.int32),
-    ]
-    near = lax.dynamic_slice_in_dim(pair_of_row, z * (COLS * NY), COLS * NY).reshape(NY, COLS)
-    left = jnp.concatenate([near, pair_picks[PG:].reshape(NY, PT)], axis=1).reshape(-1)
-    pairs = jnp.concatenate(right + [left])[:, None]
-    tx_hot = (pairs // 128 == jnp.arange(64)[None, :]).astype(BF16)
-    rx_hot = ((pairs % 128 == jnp.arange(128)[None, :]) & (pairs >= 0)).astype(BF16)
-
-    left_ids = jnp.concatenate(
-        [t * COLS + jnp.arange(COLS), lax.dynamic_slice_in_dim(picks, PG + y * PT, PT)]
-    )
-    right_ids = jnp.concatenate(
-        [picks[:PG], g * ROWS + jnp.arange(ROWS), jnp.full((RIGHT - PG - ROWS,), -1)]
-    )
-    left_damp = jnp.concatenate(
-        [
-            lax.dynamic_slice_in_dim(damping, t * COLS, COLS),
-            lax.dynamic_slice_in_dim(damp_picks, PG + y * PT, PT),
-        ]
-    )
-    damp = jnp.where(left_ids[:, None] == right_ids[None, :], left_damp[:, None], 0.0)
-
-    part = gram_sums(fields, cond, tx_hot, rx_hot)
-    return solve(part.reshape(NY, LEFT, RIGHT), damp)
 
 
 def solution(mesh):

time: 120 us -> 125 us (1.042)
  local copies, waits for them, and re-layouts: 4 us -> 9.57 us
  other arithmetic: 5.38 us -> 0 us
  Pallas kernels: 109 us -> 114 us
    broadcast_in_dim x0 -> x4, local copies, waits for them, and re-layouts: none -> 5.24 us  [the longest x1 1.31 us: shards(): tx_of_row[None, :]]
    pallas_call x2 -> x1, Pallas kernels: 109 us -> 114 us  [shards(): pl.pallas_call(step_kernel, out_shape=(jax.ShapeDtypeStruct((ROWS, COLS),...]
    reduce_sum x3 -> x0, other arithmetic: 2.52 us -> none  [the longest x1 1.22 us: shards(): damp_picks = jnp.sum(jnp.where(chosen, damping[None, :], 0.0), axis=1)]
    dynamic_slice x5 -> x0, local copies, waits for them, and re-layouts: 1.85 us -> none  [the longest x1 0.83 us: shards(): lax.dynamic_slice_in_dim(panel_order, g * PG, PG)]
    unnamed x1, local copies, waits for them, and re-layouts: 1.1 us -> 2.62 us
    concatenate x6 -> x0, other arithmetic: 1.33 us -> none  [the longest x1 1.01 us: shards(): jnp.concatenate([tx_fields, rx_fields], axis=0).reshape(2, 96, CELLS)]
where the time goes in v3:
time: 125 us; the launch traced here: 124 us
  Pallas kernels  114 us (91%)
  local copies, waits for them, and re-layouts  9.57 us (8%)
    pallas_call x1, Pallas kernels, shards(): pl.pallas_call(step_kernel, out_shape=(jax.ShapeDtypeStruct((ROWS, COLS),...  114 us
    unnamed x1, local copies, waits for them, and re-layouts  2.62 us

profile of v3, /device:TPU:16, one launch (start us, length us, event | category | flops | bytes accessed | tf_op | source)
XLA Modules:
  0.0 124.3 jit_solution(1433485332911648961)
XLA Ops:
  0.6 1.3 %broadcast_in_dim.16.tx_row_ref = s32[1,2816]{1,0:T(1,128)} reshape(s32[2816]{0:T(1024)} %param.12) | data formatting | bytes 22528 | tf_op jit(solution)/shard_map/broadcast_in_dim | solution.py:610
  1.9 1.3 %broadcast_in_dim.17.rx_row_ref = s32[1,2816]{1,0:T(1,128)} reshape(s32[2816]{0:T(1024)} %param.13) | data formatting | bytes 22528 | tf_op jit(solution)/shard_map/broadcast_in_dim | solution.py:610
  3.3 1.3 %broadcast_in_dim.18.damp_row_ref = f32[1,2816]{1,0:T(1,128)} reshape(f32[2816]{0:T(1024)} %param.14) | data formatting | bytes 22528 | tf_op jit(solution)/shard_map/broadcast_in_dim | solution.py:610
  4.6 1.3 %broadcast_in_dim.19.order_ref = s32[1,2816]{1,0:T(1,128)} reshape(s32[2816]{0:T(1024)} %param.15) | data formatting | bytes 22528 | tf_op jit(solution)/shard_map/broadcast_in_dim | solution.py:610
  5.9 114.1 %step.1 = (f32[352,88]{1,0:T(8,128)}, f32[352,1024]{1,0:T(8,128)}) custom-call(bf16[64,1024]{1,0:T(8,128)(2,1)} %tx_ref.1, bf16[128,1024]{1,0:T(8,128)(2,1)} %rx_ref.1, s32[1,1024]{1,0:T(1,128)} %bitcast.1, f32[32]{0:T(128)} %cond_ref.1, s32[1,2816]{1,0:T(1,128)} %broadcast_in_dim.16.tx_row_ref, s32[1,2816]{1,0:T(1,128)} %broadcast_in_dim.17.rx_row_ref, ...), custom_call_target="tpu_custom_call" | custom-call | tf_op jit(solution)/shard_map/step/pallas_call | solution.py:560
  120.0 1.7 %copy.10 = f32[352,88]{0,1:T(8,128)} copy(f32[352,88]{1,0:T(8,128)} %get-tuple-element.2) | data formatting | bytes 247808 | tf_op jit(solution)/shard_map/step/pallas_call | solution.py:560
  121.7 2.6 %copy.12 = f32[352,1024]{1,0:T(8,128)} copy(f32[352,1024]{1,0:T(8,128)} %get-tuple-element.7) | data formatting | bytes 2883584

commit v4 on v3

--- a/solution.py
+++ b/solution.py
@@ -68,51 +68,52 @@
 
 
 MSGS = 3
-ROW_STEP = 32
-
-
-def look_up(at, table):
-    lanes = lax.broadcasted_iota(jnp.int32, (at.shape[0], table.shape[1]), 1)
-    return jnp.sum(jnp.where(at == lanes, table, 0.0), axis=1, keepdims=True)
-
-
-def prepare(order_ref, tx_row_ref, rx_row_ref, damp_row_ref, tx_hot, rx_hot, damp, g, z, y, t):
-    order = order_ref[:, 0:PICKED].astype(F32)
-    txs, rxs = tx_row_ref[...].astype(F32), rx_row_ref[...].astype(F32)
-
-    def rows(i, carry):
-        begin = pl.multiple_of(i * ROW_STEP, ROW_STEP)
-        r = begin + lax.broadcasted_iota(jnp.int32, (ROW_STEP, 1), 0)
-        s = r - RIGHT
-        part = (s >= LEFT).astype(jnp.int32) + (s >= 2 * LEFT).astype(jnp.int32) + (s >= 3 * LEFT).astype(jnp.int32)
-        q = s - part * LEFT
-        right = s < 0
-        is_pick = (right & (r < PG)) | ((s >= 0) & (q >= COLS))
-        place = jnp.where(right, g * PG + r, (z * NY + part) * PT + q - COLS)
-        plain = jnp.where(right, g * ROWS + r - PG, (z * NY + part) * COLS + q)
-        plain = jnp.where(right & (r >= PG + ROWS), -1, plain)
-        picked = look_up(jnp.where(is_pick, place, -1), order).astype(jnp.int32)
-        ids = jnp.where(is_pick, picked, plain)
-        lanes = lax.broadcasted_iota(jnp.int32, (ROW_STEP, M), 1)
-        hit = ids == lanes
-        none = jnp.where(ids < 0, -1.0, 0.0)
-        txv = jnp.sum(jnp.where(hit, txs, 0.0), axis=1, keepdims=True) + none
-        rxv = jnp.sum(jnp.where(hit, rxs, 0.0), axis=1, keepdims=True) + none
-        here = pl.ds(begin, ROW_STEP)
-        lane = lax.broadcasted_iota(jnp.int32, (ROW_STEP, 128), 1).astype(F32)
-        tx_hot[here, :] = jnp.where(txv == lane, 1.0, 0.0).astype(BF16)
-        rx_hot[here, :] = jnp.where(rxv == lane, 1.0, 0.0).astype(BF16)
-        return carry
-
-    lax.fori_loop(0, (RIGHT + NY * LEFT) // ROW_STEP, rows, 0)
-
-    q = lax.broadcasted_iota(jnp.int32, (LEFT, 1), 0)
-    picked = look_up(jnp.where(q >= COLS, t * PT + q - COLS, -1), order).astype(jnp.int32)
-    left = jnp.where(q >= COLS, picked, t * COLS + q)
-    near = look_up(left, damp_row_ref[...])
+LINES = 24
+
+
+def look_up(ids, tables):
+    count = ids.shape[0]
+    lanes = lax.broadcasted_iota(jnp.int32, (count, 128), 1)
+    line = jnp.where((ids >> 7) == lanes, 1.0, 0.0).astype(BF16)[:, 0:LINES]
+    found = dot(line, jnp.concatenate(tables, axis=1).astype(BF16), 1, 0)
+    mine = (ids & 127) == lanes
+    return [
+        jnp.sum(jnp.where(mine, found[:, 128 * i : 128 * i + 128], 0.0), axis=1, keepdims=True)
+        for i in range(len(tables))
+    ]
+
+
+def column(row):
+    at = [lax.broadcasted_iota(jnp.int32, (128, 128), d) for d in (0, 1)]
+    return jnp.sum(jnp.where(at[0] == at[1], row, 0.0), axis=1, keepdims=True)
+
+
+def prepare(tx_list, rx_list, damp_list, order, tx_hot, rx_hot, damp, g, z, y, t):
+    def run(begin, count):
+        return begin + lax.broadcasted_iota(jnp.int32, (count, 1), 0)
+
+    right_row = order[pl.ds(g, 1), :].astype(F32)
+    left_picks = column(order[pl.ds(z, 1), :].astype(F32)).astype(jnp.int32)
+    ids = [column(right_row).astype(jnp.int32), run(g * ROWS, ROWS), run(0, RIGHT - PG - ROWS) * 0 - 1]
+    for j in range(NY):
+        ids += [run((z * NY + j) * COLS, COLS), left_picks[PT * j : PT * j + PT, :]]
+    ids = jnp.concatenate(ids, axis=0)
+    txv, rxv = look_up(ids, [v[...].astype(F32) for v in (tx_list, rx_list)])
+    none = jnp.where(ids < 0, -1.0, 0.0)
+    lane = lax.broadcasted_iota(jnp.int32, (RIGHT + NY * LEFT, 128), 1).astype(F32)
+    tx_hot[...] = jnp.where(txv + none == lane, 1.0, 0.0).astype(BF16)
+    rx_hot[...] = jnp.where(rxv + none == lane, 1.0, 0.0).astype(BF16)
+
+    own_picks = sum(jnp.where(y == j, left_picks[PT * j : PT * j + PT, :], 0) for j in range(NY))
+    left = jnp.concatenate([run(t * COLS, COLS), own_picks], axis=0)
+    table = damp_list[...]
+    high = table.astype(BF16).astype(F32)
+    mid = (table - high).astype(BF16).astype(F32)
+    terms = look_up(left, [high, mid, table - high - mid])
+    near = terms[0] + (terms[1] + terms[2])
     natural = lax.broadcasted_iota(jnp.int32, (1, GC), 1)
     natural = jnp.where(natural < ROWS, g * ROWS + natural, -1)
-    right = jnp.concatenate([order_ref[:, pl.ds(pl.multiple_of(g * PG, PG), PG)], natural], axis=1)
+    right = jnp.concatenate([right_row.astype(jnp.int32), natural], axis=1)
     damp[...] = jnp.where(left == right, near, 0.0)
 
 
@@ -171,10 +172,10 @@
     for copy in mine:
         copy.start()
     layer = layer_ref[...]
-    cond = jnp.zeros((1, CELLS), F32)
+    cond = jnp.zeros(layer.shape, F32)
     for level in range(32):
         cond = jnp.where(layer == level, cond_ref[level], cond)
-    conds[z] = cond
+    conds[z] = jnp.concatenate([cond[r : r + 1, :] for r in range(CELLS // 128)], axis=1)
     line(1).start()
     line(2).start()
     prep()
@@ -201,17 +202,10 @@
                     to_pair(n, m).wait_recv()
 
         o = owner_of(z, i)
-        width = 256
-
-        def chunk(j, carry):
-            at = pl.ds(pl.multiple_of(j * width, width), width)
-            txs = jnp.concatenate([held[o, k, 0, :, at] for k in range(NCORE)], axis=0)
-            rxs = jnp.concatenate([held[o, k, m, :, at] for k in range(NCORE) for m in (1, 2)], axis=0)
-            both = dot(tx_hot[:, 0:64], txs, 1, 0) * dot(rx_hot[...], rxs, 1, 0)
-            sens[:, at] = (both * conds[o, :, at]).astype(BF16)
-            return carry
-
-        lax.fori_loop(0, CELLS // width, chunk, 0)
+        txs = jnp.concatenate([held[o, k, 0] for k in range(NCORE)], axis=0)
+        rxs = jnp.concatenate([held[o, k, m] for k in range(NCORE) for m in (1, 2)], axis=0)
+        both = dot(tx_hot[:, 0:64], txs, 1, 0) * dot(rx_hot[...], rxs, 1, 0)
+        sens[...] = (both * conds[o]).astype(BF16)
         part[...] += dot(sens[RIGHT:, :], sens[0:RIGHT, :], 1, 1).reshape(NY, LEFT, RIGHT)
         return carry
 
@@ -311,11 +305,11 @@
 
 
 def step_kernel(
-    tx_ref, rx_ref, layer_ref, cond_ref, tx_row_ref, rx_row_ref, damp_row_ref, order_ref,
+    tx_ref, rx_ref, layer_ref, cond_ref, tx_list, rx_list, damp_list, order,
     trail_ref, factor_ref,
     part_ref, damp_ref, held, conds, sens, tx_hot, rx_hot,
     gr_send, gr_recv, gc_send, gc_recv, gp_send, gp_recv, local,
-    now, acc, nxt, high, low, wh, wl, xh, xl, got, diag, side_rows, cross, rest,
+    now, acc, nxt, high, low, wh, wl, xh, xl, got, diag, side_rows, cross,
     rs_send, rs_recv, dz_send, dz_recv, dy_send, dy_recv, dx_send, dx_recv, dp_send, dp_recv,
     cz_send, cz_recv, cy_send, cy_recv, ex_send, ex_recv, ep_send, ep_recv,
 ):
@@ -328,9 +322,7 @@
     greet(at_y[1:] + at_x[1:] + in_z[1:] + [pair])
 
     def prep():
-        prepare(
-            order_ref, tx_row_ref, rx_row_ref, damp_row_ref, tx_hot, rx_hot, damp_ref, g, z, y, z * NY + y
-        )
+        prepare(tx_list, rx_list, damp_list, order, tx_hot, rx_hot, damp_ref, g, z, y, z * NY + y)
 
     finish = gram_part(
         tx_ref, rx_ref, layer_ref, cond_ref, prep, part_ref, held, conds, sens, tx_hot, rx_hot,
@@ -527,10 +519,8 @@
     here(NG - 1)
     side(NG - 2, 6 * B)
     side(NG - 1, 7 * B)
-    rest[0:COLS, :] = summed(REST)
-    rest[COLS:, :] = jnp.zeros((B - COLS, GC), F32)
-    drop = dot3(xh[:, 0:GC], xl[:, 0:GC], xh[:, GC:], xl[:, GC:], 0, 0)
-    trail_ref[...] = (rest[...].T - drop)[0:ROWS, 0:COLS]
+    drop = dot3(xh[:, GC:], xl[:, GC:], xh[:, 0:GC], xl[:, 0:GC], 0, 0)
+    trail_ref[...] = (summed(REST) - drop[0:COLS, :])[:, 0:ROWS]
 
     finish()
     for d in range(1, NY):
@@ -555,12 +545,16 @@
 def shards(
     tx_fields, rx_fields, layer_of_cell, layer_cond, tx_of_row, rx_of_row, damping, panel_order
 ):
+    lists = [
+        jnp.pad(v, (0, LINES * 128 - M)).reshape(LINES, 128)
+        for v in (tx_of_row, rx_of_row, damping, panel_order)
+    ]
     vmem = pl.BlockSpec(memory_space=VMEM)
     smem = pl.BlockSpec(memory_space=pltpu.SMEM)
-    return pl.pallas_call(
+    trailing, factor = pl.pallas_call(
         step_kernel,
         out_shape=(
-            jax.ShapeDtypeStruct((ROWS, COLS), F32),
+            jax.ShapeDtypeStruct((COLS, ROWS), F32),
             jax.ShapeDtypeStruct((ROWS, PICKED), F32),
         ),
         in_specs=[vmem, vmem, vmem, smem, vmem, vmem, vmem, vmem],
@@ -592,7 +586,6 @@
             VMEM((NG, NZ, NY, PT, PG), F32),
             VMEM((NZ, NY, PT, GC), F32),
             VMEM((NG, COLS, PG), F32),
-            VMEM((B, GC), F32),
         ]
         + [DMA((4, NY))] * 2
         + [DMA((NZ,))] * 2
@@ -602,13 +595,13 @@
         + [DMA((NZ, NY))] * 2
         + [DMA((NX,))] * 4,
         compiler_params=pltpu.CompilerParams(
-            collective_id=0, has_side_effects=True, vmem_limit_bytes=56 << 20
+            collective_id=0, has_side_effects=True, vmem_limit_bytes=34 << 20
         ),
         name="step",
     )(
-        tx_fields, rx_fields, layer_of_cell[None, :], layer_cond,
-        tx_of_row[None, :], rx_of_row[None, :], damping[None, :], panel_order[None, :],
+        tx_fields, rx_fields, layer_of_cell.reshape(-1, 128), layer_cond, *lists,
     )
+    return trailing.T, factor
 
 
 def solution(mesh):

time: 125 us -> 114 us (0.912)
  Pallas kernels: 114 us -> 106 us
  local copies, waits for them, and re-layouts: 9.57 us -> 7.1 us
    pallas_call x1, Pallas kernels: 114 us -> 106 us  [shards(): pl.pallas_call(step_kernel, out_shape=(jax.ShapeDtypeStruct((COLS, ROWS),...]
    broadcast_in_dim x4 -> x0, local copies, waits for them, and re-layouts: 5.24 us -> none  [the longest x1 1.31 us: shards(): tx_of_row[None, :]]
    unnamed x1 -> x10, local copies, waits for them, and re-layouts: 2.62 us -> 4.95 us
    reshape x0 -> x3, local copies, waits for them, and re-layouts: none -> 2.15 us  [shards(): jnp.pad(v, (0, LINES * 128 - M)).reshape(LINES, 128)]
    pallas_call x1 -> x0, local copies, waits for them, and re-layouts: 1.7 us -> none  [shards(): pl.pallas_call(step_kernel, out_shape=(jax.ShapeDtypeStruct((ROWS, COLS),...]
where the time goes in v4:
time: 114 us; the launch traced here: 113 us
  Pallas kernels  106 us (93%)
  local copies, waits for them, and re-layouts  7.1 us (6%)
    pallas_call x1, Pallas kernels, shards(): pl.pallas_call(step_kernel, out_shape=(jax.ShapeDtypeStruct((COLS, ROWS),...  106 us
    unnamed x10, local copies, waits for them, and re-layouts  4.95 us

profile of v4, /device:TPU:16, one launch (start us, length us, event | category | flops | bytes accessed | tf_op | source)
XLA Modules:
  0.0 113.3 jit_solution(6147640043494363494)
XLA Ops:
  0.6 0.7 pad_bitcast_fusion.3.tx_list
  1.3 0.7 pad_bitcast_fusion.1.damp_list
  2.1 0.7 pad_bitcast_fusion
  2.8 0.0 copy-start
  2.8 0.9 copy-done
  3.7 0.0 copy-start.1
  3.7 0.9 copy-done.1
  4.6 0.0 copy-start.2
  4.6 0.7 copy-done.2
  5.3 0.0 copy-start.3
  5.3 0.7 copy-done.3
  6.0 105.6 %step.1 = (f32[88,352]{1,0:T(8,128)S(1)}, f32[352,1024]{1,0:T(8,128)S(1)}) custom-call(bf16[64,1024]{1,0:T(8,128)(2,1)S(1)} %copy-done.1, bf16[128,1024]{1,0:T(8,128)(2,1)S(1)} %copy-done, s32[8,128]{1,0:T(8,128)S(1)} %bitcast.11, f32[32]{0:T(128)S(1)} %copy-done.3, s32[24,128]{1,0:T(8,128)S(1)} %pad_bitcast_fusion.3.tx_list, ...), custom_call_target="tpu_custom_call" | custom-call | tf_op jit(solution)/shard_map/step/pallas_call | solution.py:554
  111.5 0.7 copy.12
  112.2 1.1 copy.13
Async XLA Ops:
  2.8 0.9 copy-start
  3.7 0.9 copy-start.1
  4.6 0.7 copy-start.2
  5.3 0.7 copy-start.3

commit v5 on v4

--- a/solution.py
+++ b/solution.py
@@ -118,7 +118,7 @@
 
 
 def gram_part(
-    tx_ref, rx_ref, layer_ref, cond_ref, prep, part, held, conds, sens, tx_hot, rx_hot,
+    tx_ref, rx_ref, layer_ref, cond_ref, prep, part, layers, held, conds, sens, tx_hot, rx_hot,
     ring_send, ring_recv, cond_send, cond_recv, pair_send, pair_recv, local,
 ):
     x, c, z, y = places()
@@ -169,9 +169,11 @@
         for m in (1, 2):
             at = 64 * core + 32 * (m - 1)
             mine.append(pltpu.make_async_copy(rx_ref.at[at : at + 32, :], held.at[z, core, m], local.at[core, m]))
+    mine.append(pltpu.make_async_copy(layer_ref, layers, local.at[0, MSGS]))
     for copy in mine:
         copy.start()
-    layer = layer_ref[...]
+    mine.pop().wait()
+    layer = layers[...]
     cond = jnp.zeros(layer.shape, F32)
     for level in range(32):
         cond = jnp.where(layer == level, cond_ref[level], cond)
@@ -245,34 +247,58 @@
         rows = [
             jnp.where(lane == j + 8 * h + sub, 1.0, jnp.where(here, 0.0, tiles[q + h])) for h in range(H)
         ]
-        pivots, inverses, solved, low = [], [], [], {}
-        for p in range(W):
+        pivots, begun, low, fixes = {}, [None] * W, {}, []
+        for p in range(0, W, 2):
             hp, s = divmod(p, 8)
-            pivot = full(cs[p, hp][s : s + 1, :])
-            inverse = 1.0 / pivot
-            pivots.append(pivot)
-            inverses.append(inverse)
-            row = full(rows[hp][s : s + 1, :])
-            solved.append(row)
-            for k in range(p + 1, W):
-                low[k, p] = full(cs[p, k // 8][k % 8 : k % 8 + 1, :]) * inverse
+            c0, c1 = cs[p, hp], cs[p + 1, hp]
+            a, b, c = full(c0[s : s + 1, :]), full(c0[s + 1 : s + 2, :]), full(c1[s + 1 : s + 2, :])
+            r = 1.0 / (a * c - b * b)
+            ar, br, cr = a * r, b * r, c * r
+            ratio = b / a
+            pivots[p], pivots[p + 1] = a, c - b * ratio
+            for k in range(p + 2, W):
+                e0 = full(cs[p, k // 8][k % 8 : k % 8 + 1, :])
+                e1 = full(cs[p + 1, k // 8][k % 8 : k % 8 + 1, :])
+                low[k, p] = cr * e0 - br * e1
+                low[k, p + 1] = ar * e1 - br * e0
                 for h in range(k // 8, H):
-                    cs[k, h] = cs[k, h] - cs[p, h] * low[k, p]
-            scaled = row * inverse
+                    cs[k, h] = cs[k, h] - (cs[p, h] * low[k, p] + cs[p + 1, h] * low[k, p + 1])
+            r0, r1 = full(rows[hp][s : s + 1, :]), full(rows[hp][s + 1 : s + 2, :])
+            x0, x1 = cr * r0 - br * r1, ar * r1 - br * r0
+            begun[p], begun[p + 1] = x0, x1
+            fixes.append((hp, s, ratio * r0))
             for h in range(hp, H):
-                if h == hp and s == 7:
+                if h == hp and s == 6:
                     continue
-                f = jnp.where(sub > s, cs[p, h], 0.0) if h == hp else cs[p, h]
-                rows[h] = rows[h] - f * scaled
+                f0, f1 = cs[p, h], cs[p + 1, h]
+                if h == hp:
+                    f0, f1 = jnp.where(sub > s + 1, f0, 0.0), jnp.where(sub > s + 1, f1, 0.0)
+                rows[h] = rows[h] - (f0 * x0 + f1 * x1)
         back = [None] * W
         for p in reversed(range(W)):
-            v = solved[p] * inverses[p]
-            for i in reversed(range(p + 1, W)):
+            v = begun[p]
+            for i in reversed(range(p // 2 * 2 + 2, W)):
                 v = v - low[i, p] * back[i]
             back[p] = v
-        for i in range(q + H, B // 8):
+        far = q + 2 * H
+        for i in range(q + H, min(far, B // 8)):
             terms = [column(tiles[i], j + p) * back[p] for p in range(W)]
             tiles[i] = jnp.where(here, 0.0, tiles[i]) - tree(terms)
+        if far < B // 8:
+            packed = []
+            for h in range(H):
+                v = back[8 * h]
+                for s in range(1, 8):
+                    v = jnp.where(sub == s, back[8 * h + s], v)
+                packed.append(v)
+            zh, zl = split(jnp.concatenate(tiles[far:], axis=0)[:, j : j + W])
+            ph, pq = split(jnp.concatenate(packed, axis=0))
+            drop = dot3(zh, zl, ph, pq, 1, 0)
+            for i in range(far, B // 8):
+                k = 8 * (i - far)
+                tiles[i] = jnp.where(here, 0.0, tiles[i]) - drop[k : k + 8, :]
+        for h, s, fix in fixes:
+            rows[h] = jnp.where(sub == s + 1, rows[h] - fix, rows[h])
         for h in range(H):
             scale = pivots[8 * h]
             for s in range(1, 8):
@@ -307,7 +333,7 @@
 def step_kernel(
     tx_ref, rx_ref, layer_ref, cond_ref, tx_list, rx_list, damp_list, order,
     trail_ref, factor_ref,
-    part_ref, damp_ref, held, conds, sens, tx_hot, rx_hot,
+    part_ref, damp_ref, layers, held, conds, sens, tx_hot, rx_hot,
     gr_send, gr_recv, gc_send, gc_recv, gp_send, gp_recv, local,
     now, acc, nxt, high, low, wh, wl, xh, xl, got, diag, side_rows, cross,
     rs_send, rs_recv, dz_send, dz_recv, dy_send, dy_recv, dx_send, dx_recv, dp_send, dp_recv,
@@ -325,7 +351,7 @@
         prepare(tx_list, rx_list, damp_list, order, tx_hot, rx_hot, damp_ref, g, z, y, z * NY + y)
 
     finish = gram_part(
-        tx_ref, rx_ref, layer_ref, cond_ref, prep, part_ref, held, conds, sens, tx_hot, rx_hot,
+        tx_ref, rx_ref, layer_ref, cond_ref, prep, part_ref, layers, held, conds, sens, tx_hot, rx_hot,
         gr_send, gr_recv, gc_send, gc_recv, gp_send, gp_recv, local,
     )
 
@@ -401,18 +427,18 @@
     diag[g, z, y] = summed(DIAG)
     for d in range(1, NZ):
         dz(d).start()
-    start_sums(PICK)
     for zz in range(NZ):
         arrived(zz, None, dz_recv, diag.at[g])
         for d in range(1, NY):
             dy(zz, d).start()
-    start_sums(CROSS)
     for zz in range(NZ):
         for d in range(1, NY):
             dy(zz, d).wait_recv()
         for d in range(1, NX):
             dx(zz, d).start()
         dp(zz, 0).start()
+    start_sums(PICK)
+    start_sums(CROSS)
     start_sums(REST)
     across(0)
     across(1)
@@ -551,17 +577,19 @@
     ]
     vmem = pl.BlockSpec(memory_space=VMEM)
     smem = pl.BlockSpec(memory_space=pltpu.SMEM)
+    hbm = pl.BlockSpec(memory_space=pltpu.HBM)
     trailing, factor = pl.pallas_call(
         step_kernel,
         out_shape=(
             jax.ShapeDtypeStruct((COLS, ROWS), F32),
             jax.ShapeDtypeStruct((ROWS, PICKED), F32),
         ),
-        in_specs=[vmem, vmem, vmem, smem, vmem, vmem, vmem, vmem],
+        in_specs=[hbm, hbm, hbm, smem, vmem, vmem, vmem, vmem],
         out_specs=(vmem, vmem),
         scratch_shapes=[
             VMEM((NY, LEFT, RIGHT), F32),
             VMEM((LEFT, RIGHT), F32),
+            VMEM((CELLS // 128, 128), jnp.int32),
             VMEM((NZ, NCORE, MSGS, 32, CELLS), BF16),
             VMEM((NZ, 1, CELLS), F32),
             VMEM((RIGHT + NY * LEFT, CELLS), BF16),
@@ -571,7 +599,7 @@
         + [DMA((NZ, MSGS))] * 2
         + [DMA((NZ,))] * 2
         + [DMA((NZ, MSGS))] * 2
-        + [DMA((NCORE, MSGS))]
+        + [DMA((NCORE, MSGS + 1))]
         + [
             VMEM((B, B), F32),
             VMEM((B, PICKED), F32),
@@ -599,7 +627,12 @@
         ),
         name="step",
     )(
-        tx_fields, rx_fields, layer_of_cell.reshape(-1, 128), layer_cond, *lists,
+        *(
+            pltpu.with_memory_space_constraint(v, pltpu.HBM)
+            for v in (tx_fields, rx_fields, layer_of_cell.reshape(-1, 128))
+        ),
+        layer_cond,
+        *lists,
     )
     return trailing.T, factor
 

time: 114 us -> 109 us (0.956)
  Pallas kernels: 106 us -> 103 us
  local copies, waits for them, and re-layouts: 7.1 us -> 4.56 us
    unnamed x10 -> x4, local copies, waits for them, and re-layouts: 4.95 us -> 2.41 us
    pallas_call x1, Pallas kernels: 106 us -> 103 us  [shards(): pl.pallas_call(step_kernel, out_shape=(jax.ShapeDtypeStruct((COLS, ROWS),...]
where the time goes in v5:
time: 109 us
  Pallas kernels  103 us (94%)
  local copies, waits for them, and re-layouts  4.56 us (4%)
    pallas_call x1, Pallas kernels, shards(): pl.pallas_call(step_kernel, out_shape=(jax.ShapeDtypeStruct((COLS, ROWS),...  103 us
    unnamed x4, local copies, waits for them, and re-layouts  2.41 us

profile of v5, /device:TPU:16, one launch (start us, length us, event | category | flops | bytes accessed | tf_op | source)
XLA Modules:
  0.0 108.7 jit_solution(14961434877540431648)
XLA Ops:
  0.6 0.7 pad_bitcast_fusion.3.tx_list
  1.3 0.7 pad_bitcast_fusion.1.damp_list
  2.1 0.7 pad_bitcast_fusion
  2.8 0.0 copy-start
  2.8 0.7 copy-done
  3.4 103.5 %step.1 = (f32[88,352]{1,0:T(8,128)S(1)}, f32[352,1024]{1,0:T(8,128)S(1)}) custom-call(bf16[64,1024]{1,0:T(8,128)(2,1)} %tx_ref.1, bf16[128,1024]{1,0:T(8,128)(2,1)} %rx_ref.1, s32[8,128]{1,0:T(8,128)} %bitcast.11, f32[32]{0:T(128)S(1)} %copy-done, s32[24,128]{1,0:T(8,128)S(1)} %pad_bitcast_fusion.3.tx_list, s32[24,128]{1,0:T(8,128)S(1)} %get-tuple-element.7.rx_list, ...), custom_call_target="tpu_custom_call" | custom-call | tf_op jit(solution)/shard_map/step/pallas_call | solution.py:581
  106.9 0.7 copy.12
  107.6 1.1 %copy.13 = f32[352,1024]{1,0:T(8,128)} copy(f32[352,1024]{1,0:T(8,128)S(1)} %get-tuple-element.11) | data formatting | bytes 2883584
Async XLA Ops:
  2.8 0.7 copy-start

commit v6 on v5

--- a/solution.py
+++ b/solution.py
@@ -88,7 +88,9 @@
     return jnp.sum(jnp.where(at[0] == at[1], row, 0.0), axis=1, keepdims=True)
 
 
-def prepare(tx_list, rx_list, damp_list, order, tx_hot, rx_hot, damp, g, z, y, t):
+def prepare(
+    tx_list, rx_list, damp_list, order, tx_hot, rx_hot, tx_pick, rx_pick, damp, g, z, y, t
+):
     def run(begin, count):
         return begin + lax.broadcasted_iota(jnp.int32, (count, 1), 0)
 
@@ -103,6 +105,10 @@
     lane = lax.broadcasted_iota(jnp.int32, (RIGHT + NY * LEFT, 128), 1).astype(F32)
     tx_hot[...] = jnp.where(txv + none == lane, 1.0, 0.0).astype(BF16)
     rx_hot[...] = jnp.where(rxv + none == lane, 1.0, 0.0).astype(BF16)
+    picks = jnp.concatenate([ids[0:PG, :], left_picks], axis=0)
+    txv, rxv = look_up(picks, [v[...].astype(F32) for v in (tx_list, rx_list)])
+    tx_pick[...] = jnp.where(txv == lane[0 : 2 * PG, :], 1.0, 0.0).astype(BF16)
+    rx_pick[...] = jnp.where(rxv == lane[0 : 2 * PG, :], 1.0, 0.0).astype(BF16)
 
     own_picks = sum(jnp.where(y == j, left_picks[PT * j : PT * j + PT, :], 0) for j in range(NY))
     left = jnp.concatenate([run(t * COLS, COLS), own_picks], axis=0)
@@ -118,7 +124,8 @@
 
 
 def gram_part(
-    tx_ref, rx_ref, layer_ref, cond_ref, prep, part, layers, held, conds, sens, tx_hot, rx_hot,
+    tx_ref, rx_ref, layer_ref, cond_ref, prep, part, diag_part, layers, held, conds, sens,
+    tx_hot, rx_hot, tx_pick, rx_pick,
     ring_send, ring_recv, cond_send, cond_recv, pair_send, pair_recv, local,
 ):
     x, c, z, y = places()
@@ -182,10 +189,21 @@
     line(2).start()
     prep()
     part[...] = jnp.zeros_like(part)
+    diag_part[...] = jnp.zeros_like(diag_part)
     for copy in mine:
         copy.wait()
     for m in range(MSGS):
         arrive(1, m)
+
+    def rows_of(o, tx_select, rx_select):
+        txs = jnp.concatenate([held[o, k, 0] for k in range(NCORE)], axis=0)
+        rxs = jnp.concatenate([held[o, k, m] for k in range(NCORE) for m in (1, 2)], axis=0)
+        both = dot(tx_select[:, 0:64], txs, 1, 0) * dot(rx_select[...], rxs, 1, 0)
+        return (both * conds[o]).astype(BF16)
+
+    def everything(o):
+        sens[...] = rows_of(o, tx_hot, rx_hot)
+        part[...] += dot(sens[RIGHT:, :], sens[0:RIGHT, :], 1, 1).reshape(NY, LEFT, RIGHT)
 
     def body(i, carry):
         for n in range(NZ - 1):
@@ -204,11 +222,9 @@
                     to_pair(n, m).wait_recv()
 
         o = owner_of(z, i)
-        txs = jnp.concatenate([held[o, k, 0] for k in range(NCORE)], axis=0)
-        rxs = jnp.concatenate([held[o, k, m] for k in range(NCORE) for m in (1, 2)], axis=0)
-        both = dot(tx_hot[:, 0:64], txs, 1, 0) * dot(rx_hot[...], rxs, 1, 0)
-        sens[...] = (both * conds[o]).astype(BF16)
-        part[...] += dot(sens[RIGHT:, :], sens[0:RIGHT, :], 1, 1).reshape(NY, LEFT, RIGHT)
+        sens_pick = rows_of(o, tx_pick, rx_pick)
+        product = dot(sens_pick[PG:, :], sens_pick[0:PG, :], 1, 1)
+        diag_part[...] += product.reshape(NY, PT, PG)
         return carry
 
     lax.fori_loop(0, NZ, body, 0)
@@ -220,7 +236,7 @@
                 to_pair(i, m).wait_send()
             line(i).wait_send()
 
-    return finish
+    return everything, finish
 
 
 def tree(vs):
@@ -333,7 +349,7 @@
 def step_kernel(
     tx_ref, rx_ref, layer_ref, cond_ref, tx_list, rx_list, damp_list, order,
     trail_ref, factor_ref,
-    part_ref, damp_ref, layers, held, conds, sens, tx_hot, rx_hot,
+    part_ref, diag_part, damp_ref, layers, held, conds, sens, tx_hot, rx_hot, tx_pick, rx_pick,
     gr_send, gr_recv, gc_send, gc_recv, gp_send, gp_recv, local,
     now, acc, nxt, high, low, wh, wl, xh, xl, got, diag, side_rows, cross,
     rs_send, rs_recv, dz_send, dz_recv, dy_send, dy_recv, dx_send, dx_recv, dp_send, dp_recv,
@@ -348,17 +364,22 @@
     greet(at_y[1:] + at_x[1:] + in_z[1:] + [pair])
 
     def prep():
-        prepare(tx_list, rx_list, damp_list, order, tx_hot, rx_hot, damp_ref, g, z, y, z * NY + y)
-
-    finish = gram_part(
-        tx_ref, rx_ref, layer_ref, cond_ref, prep, part_ref, layers, held, conds, sens, tx_hot, rx_hot,
+        prepare(
+            tx_list, rx_list, damp_list, order, tx_hot, rx_hot, tx_pick, rx_pick, damp_ref,
+            g, z, y, z * NY + y,
+        )
+
+    everything, finish = gram_part(
+        tx_ref, rx_ref, layer_ref, cond_ref, prep, part_ref, diag_part, layers, held, conds, sens,
+        tx_hot, rx_hot, tx_pick, rx_pick,
         gr_send, gr_recv, gc_send, gc_recv, gp_send, gp_recv, local,
     )
 
     def rs(p, d):
         rows, cols = PARTS[p]
+        there = lax.rem(y + d, NY)
         return sends(
-            part_ref.at[lax.rem(y + d, NY), rows, cols], got.at[d - 1, rows, cols],
+            diag_part.at[there] if p == DIAG else part_ref.at[there, rows, cols], got.at[d - 1, rows, cols],
             rs_send.at[p, d], rs_recv.at[p, d], at_y[d],
         )
 
@@ -368,7 +389,7 @@
 
     def summed(p):
         rows, cols = PARTS[p]
-        total = part_ref[y, rows, cols]
+        total = diag_part[y] if p == DIAG else part_ref[y, rows, cols]
         for d in range(1, NY):
             rs(p, d).wait_recv()
             total += got[d - 1, rows, cols]
@@ -421,38 +442,65 @@
     low[...] = jnp.zeros_like(low)
     xh[...] = jnp.zeros_like(xh)
     xl[...] = jnp.zeros_like(xl)
-    acc[...] = jnp.zeros_like(acc)
-    wh[0] = jnp.zeros((B, B), BF16)
-    wl[0] = jnp.zeros((B, B), BF16)
-    diag[g, z, y] = summed(DIAG)
-    for d in range(1, NZ):
-        dz(d).start()
-    for zz in range(NZ):
-        arrived(zz, None, dz_recv, diag.at[g])
-        for d in range(1, NY):
-            dy(zz, d).start()
-    for zz in range(NZ):
-        for d in range(1, NY):
-            dy(zz, d).wait_recv()
-        for d in range(1, NX):
-            dx(zz, d).start()
-        dp(zz, 0).start()
+
+    def remaining(i, carry):
+        everything(i)
+
+        @pl.when(i == 1)
+        def _():
+            diag[g, z, y] = summed(DIAG)
+            for d in range(1, NZ):
+                dz(d).start()
+
+        @pl.when(i == 4)
+        def _():
+            for zz in range(NZ):
+                arrived(zz, None, dz_recv, diag.at[g])
+                for d in range(1, NY):
+                    dy(zz, d).start()
+
+        @pl.when(i == 5)
+        def _():
+            for zz in range(NZ):
+                for d in range(1, NY):
+                    dy(zz, d).wait_recv()
+                for d in range(1, NX):
+                    dx(zz, d).start()
+                dp(zz, 0).start()
+
+        return carry
+
+    lax.fori_loop(0, NZ, remaining, 0)
     start_sums(PICK)
     start_sums(CROSS)
     start_sums(REST)
     across(0)
-    across(1)
     complete(0)
 
     def diag_rows(k, begin):
         return jnp.concatenate([diag[i, k].reshape(B, B) for i in range(begin, NG)], axis=1)
 
-    nxt[...] = diag_rows(0, 0)
-    now[...] = diag[0, 0].reshape(B, B)
+    fh, fl = split(inverse_factor(diag[0, 0].reshape(B, B)))
+    wh[0] = fh
+    wl[0] = fl
+    across(1)
+    across(2)
+    complete(1)
+    acc[...] = diag_rows(0, 0)
+    nxt[...] = diag_rows(1, 0)
+    fvh, fvl = split(dot3(fh, fl, *split(acc[:, B : 2 * B]), 1, 0))
+    now[...] = nxt[:, B : 2 * B] - dot3(fvh, fvl, fvh, fvl, 0, 0)
+    side_rows[z, y] = summed(PICK)
+    for d in range(1, NZ):
+        cz(d).start()
+    cross[g] = summed(CROSS)
+    for d in range(1, NX):
+        ex(d).start()
+    ep(0).start()
 
     def block(k, begin, depth):
         w = inverse_factor(now[...])
-        last = jnp.maximum(k - 1, 0)
+        last = k - 1
         cols = slice(begin * B, PICKED)
         ah, al = split(acc[:, cols])
         uh, ul = split(dot3(wh[last], wl[last], ah, al, 1, 0))
@@ -488,16 +536,6 @@
         across(k + 2)
         complete(k + 1)
 
-        @pl.when(k == 0)
-        def _():
-            side_rows[z, y] = summed(PICK)
-            for d in range(1, NZ):
-                cz(d).start()
-            cross[g] = summed(CROSS)
-            for d in range(1, NX):
-                ex(d).start()
-            ep(0).start()
-
         @pl.when(k == 2)
         def _():
             for zz in range(NZ):
@@ -536,7 +574,7 @@
         side(k - 2, 6 * B)
         return carry
 
-    lax.fori_loop(0, 4, first, 0)
+    lax.fori_loop(1, 4, first, 0)
     for d in range(NX):
         ep(d).wait_recv()
     lax.fori_loop(4, 6, second, 0)
@@ -588,6 +626,7 @@
         out_specs=(vmem, vmem),
         scratch_shapes=[
             VMEM((NY, LEFT, RIGHT), F32),
+            VMEM((NY, PT, PG), F32),
             VMEM((LEFT, RIGHT), F32),
             VMEM((CELLS // 128, 128), jnp.int32),
             VMEM((NZ, NCORE, MSGS, 32, CELLS), BF16),
@@ -595,6 +634,8 @@
             VMEM((RIGHT + NY * LEFT, CELLS), BF16),
             VMEM((RIGHT + NY * LEFT, 128), BF16),
             VMEM((RIGHT + NY * LEFT, 128), BF16),
+            VMEM((2 * PG, 128), BF16),
+            VMEM((2 * PG, 128), BF16),
         ]
         + [DMA((NZ, MSGS))] * 2
         + [DMA((NZ,))] * 2

time: 109 us -> 110 us (level)
  no operation moved by 1% of the time
where the time goes in v6:
time: 110 us; the launch traced here: 109 us
  Pallas kernels  104 us (95%)
  local copies, waits for them, and re-layouts  4.56 us (4%)
    pallas_call x1, Pallas kernels, shards(): pl.pallas_call(step_kernel, out_shape=(jax.ShapeDtypeStruct((COLS, ROWS),...  104 us
    unnamed x4, local copies, waits for them, and re-layouts  2.41 us

profile of v6, /device:TPU:16, one launch (start us, length us, event | category | flops | bytes accessed | tf_op | source)
XLA Modules:
  0.0 108.7 jit_solution(1884817025811966190)
XLA Ops:
  0.6 0.7 pad_bitcast_fusion.3.tx_list
  1.3 0.7 pad_bitcast_fusion.1.damp_list
  2.1 0.7 pad_bitcast_fusion
  2.8 0.0 copy-start
  2.8 0.7 copy-done
  3.4 103.5 %step.1 = (f32[88,352]{1,0:T(8,128)S(1)}, f32[352,1024]{1,0:T(8,128)S(1)}) custom-call(bf16[64,1024]{1,0:T(8,128)(2,1)} %tx_ref.1, bf16[128,1024]{1,0:T(8,128)(2,1)} %rx_ref.1, s32[8,128]{1,0:T(8,128)} %bitcast.11, f32[32]{0:T(128)S(1)} %copy-done, s32[24,128]{1,0:T(8,128)S(1)} %pad_bitcast_fusion.3.tx_list, s32[24,128]{1,0:T(8,128)S(1)} %get-tuple-element.7.rx_list, ...), custom_call_target="tpu_custom_call" | custom-call | tf_op jit(solution)/shard_map/step/pallas_call | solution.py:619
  107.0 0.7 copy.12
  107.6 1.1 %copy.13 = f32[352,1024]{1,0:T(8,128)} copy(f32[352,1024]{1,0:T(8,128)S(1)} %get-tuple-element.11) | data formatting | bytes 2883584
Async XLA Ops:
  2.8 0.7 copy-start

commit v7 on v5

--- a/solution.py
+++ b/solution.py
@@ -421,9 +421,6 @@
     low[...] = jnp.zeros_like(low)
     xh[...] = jnp.zeros_like(xh)
     xl[...] = jnp.zeros_like(xl)
-    acc[...] = jnp.zeros_like(acc)
-    wh[0] = jnp.zeros((B, B), BF16)
-    wl[0] = jnp.zeros((B, B), BF16)
     diag[g, z, y] = summed(DIAG)
     for d in range(1, NZ):
         dz(d).start()
@@ -441,18 +438,32 @@
     start_sums(CROSS)
     start_sums(REST)
     across(0)
-    across(1)
     complete(0)
 
     def diag_rows(k, begin):
         return jnp.concatenate([diag[i, k].reshape(B, B) for i in range(begin, NG)], axis=1)
 
-    nxt[...] = diag_rows(0, 0)
-    now[...] = diag[0, 0].reshape(B, B)
+    fh, fl = split(inverse_factor(diag[0, 0].reshape(B, B)))
+    wh[0] = fh
+    wl[0] = fl
+    across(1)
+    across(2)
+    complete(1)
+    acc[...] = diag_rows(0, 0)
+    nxt[...] = diag_rows(1, 0)
+    fvh, fvl = split(dot3(fh, fl, *split(acc[:, B : 2 * B]), 1, 0))
+    now[...] = nxt[:, B : 2 * B] - dot3(fvh, fvl, fvh, fvl, 0, 0)
+    side_rows[z, y] = summed(PICK)
+    for d in range(1, NZ):
+        cz(d).start()
+    cross[g] = summed(CROSS)
+    for d in range(1, NX):
+        ex(d).start()
+    ep(0).start()
 
     def block(k, begin, depth):
         w = inverse_factor(now[...])
-        last = jnp.maximum(k - 1, 0)
+        last = k - 1
         cols = slice(begin * B, PICKED)
         ah, al = split(acc[:, cols])
         uh, ul = split(dot3(wh[last], wl[last], ah, al, 1, 0))
@@ -488,16 +499,6 @@
         across(k + 2)
         complete(k + 1)
 
-        @pl.when(k == 0)
-        def _():
-            side_rows[z, y] = summed(PICK)
-            for d in range(1, NZ):
-                cz(d).start()
-            cross[g] = summed(CROSS)
-            for d in range(1, NX):
-                ex(d).start()
-            ep(0).start()
-
         @pl.when(k == 2)
         def _():
             for zz in range(NZ):
@@ -536,7 +537,7 @@
         side(k - 2, 6 * B)
         return carry
 
-    lax.fori_loop(0, 4, first, 0)
+    lax.fori_loop(1, 4, first, 0)
     for d in range(NX):
         ep(d).wait_recv()
     lax.fori_loop(4, 6, second, 0)

time: 109 us -> 110 us (level)
  no operation moved by 1% of the time
where the time goes in v7:
time: 110 us; the launch traced here: 109 us
  Pallas kernels  104 us (95%)
  local copies, waits for them, and re-layouts  4.56 us (4%)
    pallas_call x1, Pallas kernels, shards(): pl.pallas_call(step_kernel, out_shape=(jax.ShapeDtypeStruct((COLS, ROWS),...  104 us
    unnamed x4, local copies, waits for them, and re-layouts  2.41 us

profile of v7, /device:TPU:16, one launch (start us, length us, event | category | flops | bytes accessed | tf_op | source)
XLA Modules:
  0.0 109.2 jit_solution(5922312634602426956)
XLA Ops:
  0.6 0.7 pad_bitcast_fusion.3.tx_list
  1.3 0.7 pad_bitcast_fusion.1.damp_list
  2.1 0.7 pad_bitcast_fusion
  2.8 0.0 copy-start
  2.8 0.7 copy-done
  3.4 104.0 %step.1 = (f32[88,352]{1,0:T(8,128)S(1)}, f32[352,1024]{1,0:T(8,128)S(1)}) custom-call(bf16[64,1024]{1,0:T(8,128)(2,1)} %tx_ref.1, bf16[128,1024]{1,0:T(8,128)(2,1)} %rx_ref.1, s32[8,128]{1,0:T(8,128)} %bitcast.11, f32[32]{0:T(128)S(1)} %copy-done, s32[24,128]{1,0:T(8,128)S(1)} %pad_bitcast_fusion.3.tx_list, s32[24,128]{1,0:T(8,128)S(1)} %get-tuple-element.7.rx_list, ...), custom_call_target="tpu_custom_call" | custom-call | tf_op jit(solution)/shard_map/step/pallas_call | solution.py:582
  107.4 0.7 copy.12
  108.1 1.1 %copy.13 = f32[352,1024]{1,0:T(8,128)} copy(f32[352,1024]{1,0:T(8,128)S(1)} %get-tuple-element.11) | data formatting | bytes 2883584
Async XLA Ops:
  2.8 0.7 copy-start
